TPU v7x, 32 devices: a whole 2x2x4 slice. The times are simulated.
32 devices in a mesh: grp: 2 (over y), cell: 16 (over z, x, core).
Axes of the slice: x: 2, y: 2, z: 4, core: 2. Of those that a mesh axis runs over, the one named last changes fastest.
Arguments:
- momenta: int32 [3, 65536], replicated, may hold values from 1 to 32
- positions: float32 [3, 4096], P(None, ('grp', 'cell')), parts along dimension 1, may hold values from 0 to 1
- weights: bfloat16 [8, 4096], P(None, ('grp', 'cell')), parts along dimension 1, may hold values from 0.099609375 to 2
- triplets: int32 [3, 16384], P(None, ('grp', 'cell')), parts along dimension 1, may hold values from 0 to 65535, as said below
- cotangent: float32 [8, 16384], P(None, ('grp', 'cell')), parts along dimension 1, may hold values from -6 to 6
Outputs:
- correlation: float32 [8, 16384], P(None, ('grp', 'cell')), parts along dimension 1
- weight_grad: float32 [8, 4096], P(None, ('grp', 'cell')), parts along dimension 1
There are 2 independent parts, one for each index of `grp`. A program takes and returns all parts, laid end to end along the dimension named above; an argument that names none is the same for every part. Nothing has to cross between parts.
Inputs may be any that keep to these rules, and one draw needn't show every extreme that they name: Among the 1536 momentum indices of one device's triplets, each block of 4096 momenta (4096 * r to 4096 * r + 4095) is named either 96 - 1 or 96 times.
All inputs are finite; a program needn't handle non-finite values.
Results may differ from a plain program's by a relative error of at most 0.0051.
Values may be sent and summed in bfloat16 or wider, within the bound.
No kernel may reach another device: no remote copies, remote signals or barrier semaphores. Data moves between devices by JAX's collectives and lax.ppermute only.
A program may use at most 256 MiB of HBM per device.

v0:
```python
import math

import jax
import jax.numpy as jnp
from jax import lax
from jax.sharding import PartitionSpec as P

TWO_PI = 2.0 * math.pi


def tables(moment_block, position_block):
    numbers = moment_block.astype(jnp.float32)
    phase = numbers[0][:, None] * position_block[0][None, :]
    phase = phase + numbers[1][:, None] * position_block[1][None, :]
    phase = phase + numbers[2][:, None] * position_block[2][None, :]
    phase = TWO_PI * phase
    return (jnp.cos(phase).astype(jnp.bfloat16), jnp.sin(phase).astype(jnp.bfloat16))


def contract(left, right):
    return lax.dot_general(
        left, right, (((1,), (1,)), ((), ())), preferred_element_type=jnp.float32
    )


def amplitude_term(moment_block, position_block, weight_block):
    cosine, sine = tables(moment_block, position_block)
    return jnp.concatenate([contract(weight_block, cosine), contract(weight_block, sine)], 0)


def gradient_term(adjoint_block, moment_block, position_block):
    cosine, sine = tables(moment_block, position_block)
    bin_count = adjoint_block.shape[0] // 2
    return jnp.dot(adjoint_block[:bin_count], cosine, preferred_element_type=jnp.float32) + jnp.dot(
        adjoint_block[bin_count:], sine, preferred_element_type=jnp.float32
    )


def couple(cotangent, real_one, imag_one, real_two, imag_two):
    real_part = cotangent * (real_one * real_two - imag_one * imag_two)
    imag_part = -cotangent * (imag_one * real_two + real_one * imag_two)
    return jnp.concatenate([real_part, imag_part], 0)


def triplet_terms(amplitude, triplets, cotangent, bin_count):
    real_rows = amplitude[:bin_count]
    imag_rows = amplitude[bin_count:]
    real_a = real_rows[:, triplets[0]]
    real_b = real_rows[:, triplets[1]]
    real_c = real_rows[:, triplets[2]]
    imag_a = imag_rows[:, triplets[0]]
    imag_b = imag_rows[:, triplets[1]]
    imag_c = imag_rows[:, triplets[2]]
    correlation = (
        real_a * real_b * real_c
        - real_a * imag_b * imag_c
        - imag_a * real_b * imag_c
        - imag_a * imag_b * real_c
    )
    adjoint = jnp.zeros(amplitude.shape, jnp.float32)
    adjoint = adjoint.at[:, triplets[0]].add(couple(cotangent, real_b, imag_b, real_c, imag_c))
    adjoint = adjoint.at[:, triplets[1]].add(couple(cotangent, real_a, imag_a, real_c, imag_c))
    adjoint = adjoint.at[:, triplets[2]].add(couple(cotangent, real_a, imag_a, real_b, imag_b))
    return (correlation, adjoint)


def spread(owned_part):
    return lax.all_gather(owned_part, "cell", axis=1, tiled=True)


def on_device(momenta, positions, weights, triplets, cotangent):
    devices = lax.axis_size("cell")
    bin_count = weights.shape[0]
    moment_count = momenta.shape[1]
    local_cells = positions.shape[1]
    all_cells = local_cells * devices
    norm_factor = 1.0 / math.sqrt(all_cells)
    moment_step = min(moment_count, 4096)
    moment_blocks = moment_count // moment_step
    full_amp = None

    def forward_cells(index, buffer):
        start = index * moment_step
        moment_block = lax.dynamic_slice_in_dim(momenta, start, moment_step, 1)
        term = amplitude_term(moment_block, positions, weights)
        return lax.dynamic_update_slice_in_dim(buffer, term, start, 1)

    partial_sums = lax.fori_loop(
        0, moment_blocks, forward_cells, jnp.zeros((2 * bin_count, moment_count), jnp.float32)
    )
    owned_amp = (
        lax.psum_scatter(partial_sums, "cell", scatter_dimension=1, tiled=True) * norm_factor
    )
    amplitude = spread(owned_amp)
    correlation, adjoint = triplet_terms(amplitude, triplets, cotangent, bin_count)
    owned_sum = lax.psum_scatter(adjoint, "cell", scatter_dimension=1, tiled=True)
    owned_adjoint = (owned_sum * norm_factor).astype(jnp.bfloat16)
    full_adjoint = lax.all_gather(owned_adjoint, "cell", axis=1, tiled=True)

    def backward_cells(index, summed):
        start = index * moment_step
        moment_block = lax.dynamic_slice_in_dim(momenta, start, moment_step, 1)
        adjoint_block = lax.dynamic_slice_in_dim(full_adjoint, start, moment_step, 1)
        return summed + gradient_term(adjoint_block, moment_block, positions)

    weight_grad = lax.fori_loop(
        0, moment_blocks, backward_cells, jnp.zeros((bin_count, local_cells), jnp.float32)
    )
    return (correlation, weight_grad)


def solution(mesh):
    placed = (
        P(),
        P(None, ("grp", "cell")),
        P(None, ("grp", "cell")),
        P(None, ("grp", "cell")),
        P(None, ("grp", "cell")),
    )
    return jax.shard_map(
        on_device,
        mesh=mesh,
        in_specs=placed,
        out_specs=(P(None, ("grp", "cell")), P(None, ("grp", "cell"))),
        check_vma=False,
    )
```

profile of v0, /device:TPU:0, one launch (start us, length us, event | category | flops | bytes accessed | tf_op | source)
XLA Modules:
  0.0 1721.0 jit_solution(12182722601391225925)
XLA Ops:
  9.6 271.6 %while.27 = (s32[]{:T(128)}, f32[16,65536]{1,0:T(8,128)}, s32[3,65536]{1,0:T(4,128)}, f32[3,128]{1,0:T(4,128)S(1)}, bf16[8,128]{1,0:T(8,128)(2,1)S(1)}, /*index=5*/s32[]{:T(128)}, s32[]{:T(128)}, s32[]{:T(128)}, s32[]{:T(128)}) while((s32[]{:T(128)}, f32[16,65536]{1,0:T(8,128)}, s32[3,65536]{1,0:T(4,128)}, f32[3,128]{1,0:T(4,128)S(1)}, ...), condition=%wide.region_1.0_spmd, body=%wide.region_0.0_spmd.sunk | while | flops 24195076 | bytes 1091739 | solution.py:88
  10.5 7.7 convolution_bitcast_fusion.4
  27.4 7.7 convolution_bitcast_fusion.4
  44.4 7.7 convolution_bitcast_fusion.4
  61.4 7.7 convolution_bitcast_fusion.4
  78.3 7.7 convolution_bitcast_fusion.4
  95.3 7.7 convolution_bitcast_fusion.4
  112.3 7.7 convolution_bitcast_fusion.4
  129.2 7.7 convolution_bitcast_fusion.4
  146.1 7.7 convolution_bitcast_fusion.4
  163.1 7.7 convolution_bitcast_fusion.4
  180.0 7.7 convolution_bitcast_fusion.4
  197.0 7.7 convolution_bitcast_fusion.4
  214.0 7.7 convolution_bitcast_fusion.4
  230.9 7.7 convolution_bitcast_fusion.4
  247.9 7.7 convolution_bitcast_fusion.4
  264.8 7.7 convolution_bitcast_fusion.4
  281.2 16.9 copy.53
  298.1 333.3 %reduce-scatter.3.cloned.1.call-done = f32[16,4096]{0,1:T(8,128)} async-done(((f32[16,65536]{0,1:T(8,128)}), f32[16,4096]{0,1:T(8,128)}) %reduce-scatter.3.cloned.1.call-update) | async-done | bytes 262160 | tf_op jit(solution)/shard_map/reduce_scatter | solution.py:92
  635.4 166.6 %all-gather.3.cloned.1.call-done = f32[16,65536]{0,1:T(8,128)} async-done(((f32[16,4096]{0,1:T(8,128)}), f32[16,65536]{0,1:T(8,128)}) %all-gather.3.cloned.1.call-update) | async-done | bytes 4194320 | tf_op jit(solution)/shard_map/all_gather | solution.py:68
  802.0 44.5 %fusion.44 = (f32[8,65536]{0,1:T(8,128)}, f32[8,65536]{0,1:T(8,128)}) fusion(f32[16,65536]{0,1:T(8,128)} %all-gather.3.cloned.1.call-done), kind=kLoop, calls=%fused_computation.100 | loop fusion | bytes 8388608 | tf_op jit(solution)/shard_map/slice | solution.py:46
  846.5 11.6 gather_fusion.1
  858.0 11.6 gather_fusion
  869.6 11.6 gather_fusion.3
  881.2 11.6 gather_fusion.5
  892.8 11.6 gather_fusion.4
  904.4 11.6 gather_fusion.2
  917.4 15.4 scatter_custom_fusion
  933.0 24.6 %scatter_fusion = f32[16,65536]{0,1:T(8,128)} fusion(f32[16,65536]{0,1:T(8,128)} %scatter_custom_fusion, s32[512]{0:T(512)S(1)} %bitcast.180, f32[512,16]{1,0:T(8,128)S(1)} %copy.61), kind=kCustom, calls=%fused_computation.7 | custom fusion | flops 8192 | bytes 100352 | tf_op jit(solution)/shard_map/scatter-add | solution.py:62
  957.6 24.6 %scatter_fusion.1 = f32[16,65536]{0,1:T(8,128)} fusion(f32[16,65536]{0,1:T(8,128)} %scatter_fusion, s32[512]{0:T(512)S(1)} %bitcast.178, f32[512,16]{1,0:T(8,128)S(1)} %copy.62), kind=kCustom, calls=%fused_computation.8 | custom fusion | flops 8192 | bytes 100352 | tf_op jit(solution)/shard_map/scatter-add | solution.py:63
  982.3 330.6 %reduce-scatter.5.cloned.1.call-done = f32[16,4096]{0,1:T(8,128)} async-done(((f32[16,65536]{0,1:T(8,128)}), f32[16,4096]{0,1:T(8,128)}) %reduce-scatter.5.cloned.1.call-update) | async-done | bytes 262160 | tf_op jit(solution)/shard_map/reduce_scatter | solution.py:96
  1315.7 125.7 %all-gather.5.cloned.1.call-done = bf16[16,65536]{0,1:T(8,128)(2,1)} async-done(((bf16[16,4096]{0,1:T(8,128)(2,1)}), bf16[16,65536]{0,1:T(8,128)(2,1)}) %all-gather.5.cloned.1.call-update) | async-done | bytes 2097168 | tf_op jit(solution)/shard_map/all_gather | solution.py:98
  1441.4 12.8 copy.63
  1454.2 259.5 %while.28 = (s32[]{:T(128)}, f32[8,128]{1,0:T(8,128)S(1)}, bf16[16,65536]{1,0:T(8,128)(2,1)S(1)}, s32[3,65536]{1,0:T(4,128)}, f32[3,128]{1,0:T(4,128)S(1)}, /*in...) while((s32[]{:T(128)}, f32[8,128]{1,0:T(8,128)S(1)}, bf16[16,65536]{1,0:T(8,128)(2,1)S(1)}, ...), condition=%wide.region_8.0_spmd.clone, body=%wide.region_7.0_spmd.clone.sunk | while | flops 24132616 | bytes 448705 | solution.py:106
  1455.3 7.6 fusion.61
  1462.9 7.7 fusion.62
  1471.5 7.6 fusion.61
  1479.1 7.7 fusion.62
  1487.7 7.6 fusion.61
  1495.3 7.7 fusion.62
  1503.9 7.6 fusion.61
  1511.5 7.7 fusion.62
  1520.1 7.6 fusion.61
  1527.7 7.7 fusion.62
  1536.3 7.6 fusion.61
  1543.9 7.7 fusion.62
  1552.5 7.6 fusion.61
  1560.1 7.7 fusion.62
  1568.7 7.6 fusion.61
  1576.3 7.7 fusion.62
  1584.9 7.6 fusion.61
  1592.6 7.7 fusion.62
  1601.1 7.6 fusion.61
  1608.8 7.7 fusion.62
  1617.3 7.6 fusion.61
  1625.0 7.7 fusion.62
  1633.5 7.6 fusion.61
  1641.2 7.7 fusion.62
  1649.7 7.6 fusion.61
  1657.4 7.7 fusion.62
  1665.9 7.6 fusion.61
  1673.6 7.7 fusion.62
  1689.8 7.7 fusion.62
  1706.0 7.7 fusion.62
  (168 shorter events, 189.1 us)
Async XLA Ops:
  7.2 624.3 %reduce-scatter.3.cloned.1.call-start = ((), (), s32[]{:S(2)}) async-start(), calls=%async_computation.2 | async-start | bytes 35651584 | tf_op jit(solution)/shard_map/reduce_scatter | solution.py:92
  7.2 2.4 copy-start
  7.2 2.4 copy-start.3
  298.1 503.9 %all-gather.3.cloned.1.call-start = ((), (), s32[]{:S(2)}) async-start(), calls=%async_computation.3 | async-start | bytes 35651584 | tf_op jit(solution)/shard_map/all_gather | solution.py:68
  634.6 0.7 copy-start.2
  634.7 678.3 %reduce-scatter.5.cloned.1.call-start = ((), (), s32[]{:S(2)}) async-start(), calls=%async_computation.4 | async-start | bytes 35651584 | tf_op jit(solution)/shard_map/reduce_scatter | solution.py:96
  846.5 70.1 %copy-start.1 = (f32[8,512]{1,0:T(8,128)S(1)}, f32[8,512]{1,0:T(8,128)}, u32[]{:S(2)}) copy-start(f32[8,512]{1,0:T(8,128)} %param.13) | copy-start | bytes 49156
  982.3 459.1 %all-gather.5.cloned.1.call-start = ((), (), s32[]{:S(2)}) async-start(), calls=%async_computation.5 | async-start | bytes 17825792 | tf_op jit(solution)/shard_map/all_gather | solution.py:98
  1713.7 0.6 copy-start.4
Sparse Core Ops, SparseCore 0:
  298.2 333.2 reduce-scatter.2
  634.8 167.1 all-gather.2
  982.4 330.4 reduce-scatter.4
  1315.8 125.5 all-gather.4
where the time goes:
time: 1730 us; the launch traced here: 1720 us
  waiting for transfers between devices  956 us (55%)
  matrix products  490 us (28%)
  local copies, waits for them, and re-layouts  149 us (9%)
  other arithmetic  110 us (6%)
    reduce_scatter x1, waiting for transfers between devices, on_device(): lax.psum_scatter(partial_sums, 'cell', scatter_dimension=1, tiled=True)  333 us
    reduce_scatter x1, waiting for transfers between devices, on_device(): lax.psum_scatter(adjoint, 'cell', scatter_dimension=1, tiled=True)  331 us
    dot_general x32, matrix products, contract(): lax.dot_general(left, right, (((1,), (1,)), ((), ())), preferred_element_...  245 us
    all_gather x1, waiting for transfers between devices, spread(): return lax.all_gather(owned_part, 'cell', axis=1, tiled=True)  167 us
    all_gather x1, waiting for transfers between devices, on_device(): full_adjoint = lax.all_gather(owned_adjoint, 'cell', axis=1, tiled=True)  126 us
    dot_general x16, matrix products, gradient_term(): jnp.dot(adjoint_block[bin_count:], sine, preferred_element_type=jnp.float32)  123 us
    dot_general x16, matrix products, gradient_term(): jnp.dot(adjoint_block[:bin_count], cosine, preferred_element_type=jnp.flo...  122 us
    slice x1, local copies, waits for them, and re-layouts, triplet_terms(): real_rows = amplitude[:bin_count]  44.5 us
  transfers between devices with their start and end apart: 4, of which 4 were waited for; matrix products, arithmetic and copies ran while one was open for 0% of the time, Pallas kernels for 0%

commit v1 on v0

v1 whole, which is shorter than its diff:
```python
import functools
import math

import jax
import jax.numpy as jnp
import numpy as np
from jax import lax
from jax.experimental import pallas as pl
from jax.experimental.pallas import tpu as pltpu
from jax.sharding import PartitionSpec as P

LANES = 128
ROWS = 16
DEPTH = 32
CELL_STEP = 256
SLOT_STEP = 256
KEEP_BYTES = 24 << 20


def fit(values, terms):
    nodes = 0.125 + 0.125 * np.cos(np.pi * (np.arange(64) + 0.5) / 64)
    series = np.polynomial.chebyshev.Chebyshev.fit(nodes, values(np.sqrt(nodes)), terms - 1, domain=[0.0, 0.25])
    return [float(c) for c in series.convert(kind=np.polynomial.Polynomial).coef]


SINE = fit(lambda f: math.sqrt(2.0) * np.sin(np.pi * f) / f, 4)
COSINE = fit(lambda f: math.sqrt(2.0) * np.cos(np.pi * f), 5)


def series_of(u, coefficients):
    total = coefficients[-1] * u + coefficients[-2]
    for c in coefficients[-3::-1]:
        total = total * u + c
    return total


def cos_sin(turns):
    f = turns - jnp.round(turns)
    u = f * f
    s = f * series_of(u, SINE)
    c = series_of(u, COSINE)
    return 1.0 - s * s, s * c


def lookup_kernel(tri_ref, table_ref, out_ref):
    rows = table_ref.shape[0]
    width = tri_ref.shape[1]
    lane_iota = lax.broadcasted_iota(jnp.int32, (LANES, width), 0)
    row_iota = lax.broadcasted_iota(jnp.int32, (rows, width), 0)
    parts = [table_ref[:, d, :].astype(jnp.float32).astype(jnp.bfloat16) for d in range(3)]
    for place in range(3):
        index = tri_ref[place : place + 1, :]
        pick = jnp.where(lane_iota == (index & (LANES - 1)), 1.0, 0.0).astype(jnp.bfloat16)
        hit = row_iota == (index >> 7)
        found = []
        for d in range(3):
            line = jnp.dot(parts[d], pick, preferred_element_type=jnp.float32)
            found.append(jnp.sum(jnp.where(hit, line, 0.0), axis=0, keepdims=True))
        found.append(jnp.zeros((5, width), jnp.float32))
        eight = jnp.concatenate(found, axis=0)
        wide = jnp.concatenate([eight, eight, eight, jnp.zeros((LANES - 24, width), jnp.float32)], axis=0)
        out_ref[place * width : (place + 1) * width, :] = wide.T.astype(jnp.bfloat16)


def main_kernel(keep, norm, data_ref, slot_ref, cot_ref, corr_ref, grad_ref, x_ref, w_ref, turn_ref, cos_ref, sin_ref):
    blocks = data_ref.shape[0]
    slots = slot_ref.shape[0]
    width = cot_ref.shape[1]
    cells = blocks * LANES
    cell_steps = cells // CELL_STEP
    slot_steps = slots // SLOT_STEP
    per_step = CELL_STEP // LANES

    def prepare(j, carry):
        at = pl.ds(pl.multiple_of(j * LANES, LANES), LANES)
        place = data_ref[j, 0:8, :]
        place = place - jnp.round(place)
        high = place.astype(jnp.bfloat16).astype(jnp.float32)
        rest = place - high
        middle = rest.astype(jnp.bfloat16).astype(jnp.float32)
        low = rest - middle
        x_ref[:, at] = jnp.concatenate([high, middle, low, jnp.zeros_like(low)], axis=0).astype(jnp.bfloat16)
        w_ref[:, at] = data_ref[j, 8:16, :].astype(jnp.bfloat16)
        return carry

    lax.fori_loop(0, blocks, prepare, 0)

    def fill(step, slot_at):
        at = pl.ds(pl.multiple_of(step * CELL_STEP, CELL_STEP), CELL_STEP)
        to = pl.ds(pl.multiple_of(slot_at * CELL_STEP, CELL_STEP), CELL_STEP)
        x = x_ref[:, at]

        def some(b, carry):
            base = pl.multiple_of(b * SLOT_STEP, SLOT_STEP)
            turn_ref[...] = jnp.dot(slot_ref[pl.ds(base, SLOT_STEP), 0:DEPTH], x, preferred_element_type=jnp.float32)
            for r in range(0, SLOT_STEP, 16):
                c, s = cos_sin(turn_ref[r : r + 16, :])
                here = pl.ds(pl.multiple_of(base + r, 16), 16)
                cos_ref[here, to] = c.astype(jnp.bfloat16)
                sin_ref[here, to] = s.astype(jnp.bfloat16)
            return carry

        lax.fori_loop(0, slot_steps, some, 0)
        return at, to

    def over_slots(left, right):
        return lax.dot_general(left, right, (((1,), (1,)), ((), ())), preferred_element_type=jnp.float32)

    def forward(step, sums):
        at, to = fill(step, step if keep else 0)
        w = w_ref[:, at]
        return sums[0] + over_slots(w, cos_ref[:, to]), sums[1] + over_slots(w, sin_ref[:, to])

    zero = jnp.zeros((8, slots), jnp.float32)
    real, imag = lax.fori_loop(0, cell_steps, forward, (zero, zero))
    real, imag = real * norm, imag * norm
    ar, br, cr = (real[:, p * width : (p + 1) * width] for p in range(3))
    ai, bi, ci = (imag[:, p * width : (p + 1) * width] for p in range(3))
    cot = cot_ref[...]
    bcr, bci = br * cr - bi * ci, br * ci + bi * cr
    corr_ref[...] = ar * bcr - ai * bci
    acr, aci = ar * cr - ai * ci, ar * ci + ai * cr
    abr, abi = ar * br - ai * bi, ar * bi + ai * br
    scaled = cot * norm
    left_real = jnp.concatenate([scaled * bcr, scaled * acr, scaled * abr], axis=1).astype(jnp.bfloat16)
    left_imag = jnp.concatenate([-scaled * bci, -scaled * aci, -scaled * abi], axis=1).astype(jnp.bfloat16)

    def backward(step, carry):
        if keep:
            to = pl.ds(pl.multiple_of(step * CELL_STEP, CELL_STEP), CELL_STEP)
        else:
            _, to = fill(step, 0)
        out = jnp.dot(left_real, cos_ref[:, to], preferred_element_type=jnp.float32) + jnp.dot(
            left_imag, sin_ref[:, to], preferred_element_type=jnp.float32
        )
        for i in range(per_step):
            grad_ref[step * per_step + i] = out[:, i * LANES : (i + 1) * LANES]
        return carry

    lax.fori_loop(0, cell_steps, backward, 0)


def lookup(triplets, momenta):
    count = momenta.shape[1]
    table = momenta.reshape(3, count // LANES, LANES).transpose(1, 0, 2)
    slots = 3 * triplets.shape[1]
    return pl.pallas_call(
        lookup_kernel, out_shape=jax.ShapeDtypeStruct((slots, LANES), jnp.bfloat16), name="lookup"
    )(triplets, table)


def triplet_stage(data, slot_rows, cotangent):
    blocks = data.shape[0]
    slots = slot_rows.shape[0]
    cells = blocks * LANES
    keep = 4 * slots * cells <= KEEP_BYTES
    kept = cells if keep else CELL_STEP
    return pl.pallas_call(
        functools.partial(main_kernel, keep, 1.0 / math.sqrt(cells)),
        out_shape=(
            jax.ShapeDtypeStruct(cotangent.shape, jnp.float32),
            jax.ShapeDtypeStruct((blocks, 8, LANES), jnp.float32),
        ),
        scratch_shapes=[
            pltpu.VMEM((DEPTH, cells), jnp.bfloat16),
            pltpu.VMEM((8, cells), jnp.bfloat16),
            pltpu.VMEM((SLOT_STEP, CELL_STEP), jnp.float32),
            pltpu.VMEM((slots, kept), jnp.bfloat16),
            pltpu.VMEM((slots, kept), jnp.bfloat16),
        ],
        name="triplet_stage",
    )(data, slot_rows, cotangent)


def strides(devices):
    return [1 << i for i in range(devices.bit_length() - 1)]


def gather_cells(block, devices):
    held = block[None]
    for stride in strides(devices):
        pairs = [(i, i ^ stride) for i in range(devices)]
        held = jnp.concatenate([held, lax.ppermute(held, "cell", pairs)], axis=0)
    return held


def reduce_cells(blocks, devices):
    for stride in reversed(strides(devices)):
        pairs = [(i, i ^ stride) for i in range(devices)]
        blocks = blocks[:stride] + lax.ppermute(blocks[stride:], "cell", pairs)
    return blocks[0]


def on_device(momenta, positions, weights, triplets, cotangent):
    devices = lax.axis_size("cell")
    block = jnp.concatenate(
        [positions, jnp.zeros((5, positions.shape[1]), jnp.float32), weights.astype(jnp.float32)], axis=0
    )
    data = gather_cells(block, devices)
    slot_rows = lookup(triplets, momenta)
    correlation, partial = triplet_stage(data, slot_rows, cotangent)
    return correlation, reduce_cells(partial, devices)


def solution(mesh):
    split = P(None, ("grp", "cell"))
    return jax.shard_map(
        on_device,
        mesh=mesh,
        in_specs=(P(), split, split, split, split),
        out_specs=(split, split),
        check_vma=False,
    )
```

time: 1730 us -> 61.6 us (0.04)
  waiting for transfers between devices: 956 us -> 12.8 us
  matrix products: 490 us -> 0 us
  local copies, waits for them, and re-layouts: 149 us -> 2.18 us
  other arithmetic: 110 us -> 1.45 us
  Pallas kernels: 0 us -> 29.3 us
    reduce_scatter x2 -> x0, waiting for transfers between devices: 664 us -> none  [the longest x1 333 us: on_device(): lax.psum_scatter(partial_sums, 'cell', scatter_dimension=1, tiled=True)]
    dot_general x64 -> x0, matrix products: 490 us -> none  [the longest x32 245 us: contract(): lax.dot_general(left, right, (((1,), (1,)), ((), ())), preferred_element_...]
    all_gather x2 -> x0, waiting for transfers between devices: 292 us -> none  [the longest x1 167 us: spread(): return lax.all_gather(owned_part, 'cell', axis=1, tiled=True)]
    gather x12 -> x0, local copies, waits for them, and re-layouts: 70.1 us -> none  [the longest x2 11.7 us: triplet_terms(): real_a = real_rows[:, triplets[0]]]
    scatter-add x3 -> x0, other arithmetic: 64.6 us -> none  [the longest x1 24.6 us: triplet_terms(): adjoint.at[:, triplets[1]]]
    slice x33 -> x4, local copies, waits for them, and re-layouts: 45.6 us -> 0.85 us  [reduce_cells(): blocks = blocks[:stride] + lax.ppermute(blocks[stride:], 'cell', pairs)]
    convert_element_type x33 -> x1, other arithmetic: 30.1 us -> 0.68 us  [on_device(): weights.astype(jnp.float32)]
    pallas_call x0 -> x2, Pallas kernels: none -> 29.3 us  [the longest x1 24.6 us: triplet_stage(): pl.pallas_call(functools.partial(main_kernel, keep, 1.0 / math.sqrt(cells...]
  transfers between devices with their start and end apart: 4 -> 8, of which waited for: 4 -> 7; matrix products, arithmetic and copies ran while one was open for 0% -> 0% of each run, Pallas kernels for 0% -> 8%
where the time goes in v1:
time: 61.6 us; the launch traced here: 61.3 us
  Pallas kernels  29.3 us (48%)
  starting transfers between devices  15 us (24%)
  waiting for transfers between devices  12.8 us (21%)
  local copies, waits for them, and re-layouts  2.18 us (4%)
  other arithmetic  1.45 us (2%)
  between operations  0.66 us (1%)
    pallas_call x1, Pallas kernels, triplet_stage(): pl.pallas_call(functools.partial(main_kernel, keep, 1.0 / math.sqrt(cells...  24.6 us
    ppermute x4, starting transfers between devices, gather_cells(): held = jnp.concatenate([held, lax.ppermute(held, 'cell', pairs)], axis=0)  8.12 us
    ppermute x4, waiting for transfers between devices, reduce_cells(): blocks = blocks[:stride] + lax.ppermute(blocks[stride:], 'cell', pairs)  6.91 us
    ppermute x4, starting transfers between devices, reduce_cells(): blocks = blocks[:stride] + lax.ppermute(blocks[stride:], 'cell', pairs)  6.84 us
    ppermute x4, waiting for transfers between devices, gather_cells(): held = jnp.concatenate([held, lax.ppermute(held, 'cell', pairs)], axis=0)  5.84 us
    pallas_call x1, Pallas kernels, lookup(): pl.pallas_call(lookup_kernel, out_shape=jax.ShapeDtypeStruct((slots, LANE...  4.69 us
    unnamed x9, local copies, waits for them, and re-layouts  1.25 us
  transfers between devices with their start and end apart: 8, of which 7 were waited for; matrix products, arithmetic and copies ran while one was open for 0% of the time, Pallas kernels for 8%

profile of v1, /device:TPU:0, one launch (start us, length us, event | category | flops | bytes accessed | tf_op | source)
XLA Modules:
  0.0 61.3 jit_solution(465472089798412182)
XLA Ops:
  0.6 0.7 %convert_element_type.3 = f32[8,128]{1,0:T(8,128)S(1)} convert(bf16[8,128]{1,0:T(8,128)(2,1)} %param.7) | non-fusion elementwise | flops 1024 | bytes 6144 | tf_op jit(solution)/shard_map/convert_element_type | solution.py:197
  1.3 0.0 copy-start.2
  1.3 0.1 pad.10.clone
  1.4 0.6 copy-done.2
  2.0 0.1 maximum_bitcast_fusion
  2.1 0.5 collective-permute-start
  2.6 0.1 constant_dynamic-update-slice_fusion.4
  2.6 4.7 %lookup.1.slot_ref = bf16[1536,128]{1,0:T(8,128)(2,1)} custom-call(s32[3,512]{1,0:T(4,128)} %tri_ref.1, s32[512,3,128]{2,1,0:T(4,128)} %bitcast.9), custom_call_target="tpu_custom_call" | custom-call | tf_op jit(solution)/shard_map/lookup/pallas_call | solution.py:147
  7.3 0.0 collective-permute-done
  7.3 2.5 %collective-permute-start.1 = (f32[2,16,128]{2,1,0:T(8,128)S(1)}, f32[2,16,128]{2,1,0:T(8,128)S(1)}, u32[]{:S(2)}, u32[]{:S(2)}) collective-permute-start(f32[2,16,128]{2,1,0:T(8,128)S(1)} %pad_maximum_fusion.2), channel_id=1, source_target_pairs={{0,2},{1,3},{2,0},{3,1},{4,6},{5,7},{6,4},{7,5},{8,10},{9,11},{10,... | collective-permute-start | bytes 49160 | tf_op jit(solution)/shard_map/ppermute | solution.py:183
  9.8 1.7 %collective-permute-done.1 = f32[2,16,128]{2,1,0:T(8,128)S(1)} collective-permute-done((f32[2,16,128]{2,1,0:T(8,128)S(1)}, f32[2,16,128]{2,1,0:T(8,128)S(1)}, u32[]{:S(2)}, u32[]{:S(2)}) %collective-permute-start.1) | collective-permute-done | bytes 16416 | tf_op jit(solution)/shard_map/ppermute | solution.py:183
  11.5 2.1 %collective-permute-start.2 = (f32[4,16,128]{2,1,0:T(8,128)S(1)}, f32[4,16,128]{2,1,0:T(8,128)S(1)}, u32[]{:S(2)}, u32[]{:S(2)}) collective-permute-start(f32[4,16,128]{2,1,0:T(8,128)S(1)} %pad_maximum_fusion.1), channel_id=1, source_target_pairs={{0,4},{1,5},{2,6},{3,7},{4,0},{5,1},{6,2},{7,3},{8,12},{9,13},{10,... | collective-permute-start | bytes 98312 | tf_op jit(solution)/shard_map/ppermute | solution.py:183
  13.6 1.9 %collective-permute-done.2 = f32[4,16,128]{2,1,0:T(8,128)S(1)} collective-permute-done((f32[4,16,128]{2,1,0:T(8,128)S(1)}, f32[4,16,128]{2,1,0:T(8,128)S(1)}, u32[]{:S(2)}, u32[]{:S(2)}) %collective-permute-start.2) | collective-permute-done | bytes 32800 | tf_op jit(solution)/shard_map/ppermute | solution.py:183
  15.5 3.0 %collective-permute-start.3 = (f32[8,16,128]{2,1,0:T(8,128)S(1)}, f32[8,16,128]{2,1,0:T(8,128)S(1)}, u32[]{:S(2)}, u32[]{:S(2)}) collective-permute-start(f32[8,16,128]{2,1,0:T(8,128)S(1)} %pad_maximum_fusion), channel_id=1, source_target_pairs={{0,8},{1,9},{2,10},{3,11},{4,12},{5,13},{6,14},{7,15},{8,0},{9,1},... | collective-permute-start | bytes 196616 | tf_op jit(solution)/shard_map/ppermute | solution.py:183
  18.6 2.2 %collective-permute-done.3 = f32[8,16,128]{2,1,0:T(8,128)S(1)} collective-permute-done((f32[8,16,128]{2,1,0:T(8,128)S(1)}, f32[8,16,128]{2,1,0:T(8,128)S(1)}, u32[]{:S(2)}, u32[]{:S(2)}) %collective-permute-start.3) | collective-permute-done | bytes 65568 | tf_op jit(solution)/shard_map/ppermute | solution.py:183
  20.8 0.0 copy-start
  20.8 0.6 %copy-done = f32[16,16,128]{2,1,0:T(8,128)} copy-done((f32[16,16,128]{2,1,0:T(8,128)}, f32[16,16,128]{2,1,0:T(8,128)S(1)}, u32[]{:S(2)}) %copy-start) | copy-done | bytes 131096
  21.5 24.6 %triplet_stage.1 = (f32[8,512]{1,0:T(8,128)}, f32[16,8,128]{2,1,0:T(8,128)}) custom-call(f32[16,16,128]{2,1,0:T(8,128)} %copy-done, bf16[1536,128]{1,0:T(8,128)(2,1)} %lookup.1.slot_ref, f32[8,512]{1,0:T(8,128)} %cot_ref.1), custom_call_target="tpu_custom_call" | custom-call | tf_op jit(solution)/shard_map/triplet_stage/pallas_call | solution.py:158
  46.1 0.0 copy-start.1
  46.1 0.8 %slice.25 = f32[8,8,128]{2,1,0:T(8,128)S(1)} slice(f32[16,8,128]{2,1,0:T(8,128)} %get-tuple-element.5), slice={[8:16], [0:8], [0:128]} | slice | bytes 65536 | tf_op jit(solution)/shard_map/slice | solution.py:190
  46.9 3.0 %collective-permute-start.4 = (f32[8,8,128]{2,1,0:T(8,128)S(1)}, f32[8,8,128]{2,1,0:T(8,128)S(1)}, u32[]{:S(2)}, u32[]{:S(2)}) collective-permute-start(f32[8,8,128]{2,1,0:T(8,128)S(1)} %slice.25), channel_id=1, source_target_pairs={{0,8},{1,9},{2,10},{3,11},{4,12},{5,13},{6,14},{7,15},{8,0},{9,1},... | collective-permute-start | bytes 98312 | tf_op jit(solution)/shard_map/ppermute | solution.py:190
  49.9 1.9 %collective-permute-done.4 = f32[8,8,128]{2,1,0:T(8,128)S(1)} collective-permute-done((f32[8,8,128]{2,1,0:T(8,128)S(1)}, f32[8,8,128]{2,1,0:T(8,128)S(1)}, u32[]{:S(2)}, u32[]{:S(2)}) %collective-permute-start.4) | collective-permute-done | bytes 32800 | tf_op jit(solution)/shard_map/ppermute | solution.py:190
  51.8 0.0 copy-done.1
  51.8 2.3 %collective-permute-start.5 = (f32[4,8,128]{2,1,0:T(8,128)S(1)}, f32[4,8,128]{2,1,0:T(8,128)S(1)}, u32[]{:S(2)}, u32[]{:S(2)}) collective-permute-start(f32[4,8,128]{2,1,0:T(8,128)S(1)} %slice.33), channel_id=1, source_target_pairs={{0,4},{1,5},{2,6},{3,7},{4,0},{5,1},{6,2},{7,3},{8,12},{9,13},{10,... | collective-permute-start | bytes 49160 | tf_op jit(solution)/shard_map/ppermute | solution.py:190
  54.2 1.7 %collective-permute-done.5 = f32[4,8,128]{2,1,0:T(8,128)S(1)} collective-permute-done((f32[4,8,128]{2,1,0:T(8,128)S(1)}, f32[4,8,128]{2,1,0:T(8,128)S(1)}, u32[]{:S(2)}, u32[]{:S(2)}) %collective-permute-start.5) | collective-permute-done | bytes 16416 | tf_op jit(solution)/shard_map/ppermute | solution.py:190
  55.9 1.5 %collective-permute-start.6 = (f32[2,8,128]{2,1,0:T(8,128)S(1)}, f32[2,8,128]{2,1,0:T(8,128)S(1)}, u32[]{:S(2)}, u32[]{:S(2)}) collective-permute-start(f32[2,8,128]{2,1,0:T(8,128)S(1)} %slice.35), channel_id=1, source_target_pairs={{0,2},{1,3},{2,0},{3,1},{4,6},{5,7},{6,4},{7,5},{8,10},{9,11},{10,... | collective-permute-start | bytes 24584 | tf_op jit(solution)/shard_map/ppermute | solution.py:190
  57.4 2.1 %collective-permute-done.6 = f32[2,8,128]{2,1,0:T(8,128)S(1)} collective-permute-done((f32[2,8,128]{2,1,0:T(8,128)S(1)}, f32[2,8,128]{2,1,0:T(8,128)S(1)}, u32[]{:S(2)}, u32[]{:S(2)}) %collective-permute-start.6) | collective-permute-done | bytes 8224 | tf_op jit(solution)/shard_map/ppermute | solution.py:190
  59.6 0.0 collective-permute-start.7
  59.6 1.2 %collective-permute-done.7 = f32[1,8,128]{2,1,0:T(8,128)S(1)} collective-permute-done((f32[1,8,128]{2,1,0:T(8,128)S(1)}, f32[1,8,128]{2,1,0:T(8,128)S(1)}, u32[]{:S(2)}, u32[]{:S(2)}) %collective-permute-start.7) | collective-permute-done | bytes 4128 | tf_op jit(solution)/shard_map/ppermute | solution.py:190
  60.7 0.6 fusion
  (14 shorter events, 0.1 us)
Async XLA Ops:
  1.3 0.7 %copy-start.2 = (f32[3,128]{1,0:T(4,128)S(1)}, f32[3,128]{1,0:T(4,128)}, u32[]{:S(2)}) copy-start(f32[3,128]{1,0:T(4,128)} %param.6) | copy-start | bytes 4612
  2.1 5.3 %collective-permute-start = (f32[1,16,128]{2,1,0:T(8,128)S(1)}, f32[1,16,128]{2,1,0:T(8,128)S(1)}, u32[]{:S(2)}, u32[]{:S(2)}) collective-permute-start(f32[1,16,128]{2,1,0:T(8,128)S(1)} %maximum_bitcast_fusion), channel_id=1, source_target_pairs={{0,1},{1,0},{2,3},{3,2},{4,5},{5,4},{6,7},{7,6},{8,9},{9,8},{10,11... | collective-permute-start | bytes 24584 | tf_op jit(solution)/shard_map/ppermute | solution.py:183
  7.3 4.2 %collective-permute-start.1 = (f32[2,16,128]{2,1,0:T(8,128)S(1)}, f32[2,16,128]{2,1,0:T(8,128)S(1)}, u32[]{:S(2)}, u32[]{:S(2)}) collective-permute-start(f32[2,16,128]{2,1,0:T(8,128)S(1)} %pad_maximum_fusion.2), channel_id=1, source_target_pairs={{0,2},{1,3},{2,0},{3,1},{4,6},{5,7},{6,4},{7,5},{8,10},{9,11},{10,... | collective-permute-start | bytes 49160 | tf_op jit(solution)/shard_map/ppermute | solution.py:183
  11.5 4.0 %collective-permute-start.2 = (f32[4,16,128]{2,1,0:T(8,128)S(1)}, f32[4,16,128]{2,1,0:T(8,128)S(1)}, u32[]{:S(2)}, u32[]{:S(2)}) collective-permute-start(f32[4,16,128]{2,1,0:T(8,128)S(1)} %pad_maximum_fusion.1), channel_id=1, source_target_pairs={{0,4},{1,5},{2,6},{3,7},{4,0},{5,1},{6,2},{7,3},{8,12},{9,13},{10,... | collective-permute-start | bytes 98312 | tf_op jit(solution)/shard_map/ppermute | solution.py:183
  15.5 5.3 %collective-permute-start.3 = (f32[8,16,128]{2,1,0:T(8,128)S(1)}, f32[8,16,128]{2,1,0:T(8,128)S(1)}, u32[]{:S(2)}, u32[]{:S(2)}) collective-permute-start(f32[8,16,128]{2,1,0:T(8,128)S(1)} %pad_maximum_fusion), channel_id=1, source_target_pairs={{0,8},{1,9},{2,10},{3,11},{4,12},{5,13},{6,14},{7,15},{8,0},{9,1},... | collective-permute-start | bytes 196616 | tf_op jit(solution)/shard_map/ppermute | solution.py:183
  20.8 0.6 %copy-start = (f32[16,16,128]{2,1,0:T(8,128)}, f32[16,16,128]{2,1,0:T(8,128)S(1)}, u32[]{:S(2)}) copy-start(f32[16,16,128]{2,1,0:T(8,128)S(1)} %constant_dynamic-update-slice_fusion.data_ref) | copy-start | bytes 393220
  46.1 5.7 %copy-start.1 = (f32[16,8,128]{2,1,0:T(8,128)S(1)}, f32[16,8,128]{2,1,0:T(8,128)}, u32[]{:S(2)}) copy-start(f32[16,8,128]{2,1,0:T(8,128)} %get-tuple-element.5) | copy-start | bytes 196612
  46.9 4.9 %collective-permute-start.4 = (f32[8,8,128]{2,1,0:T(8,128)S(1)}, f32[8,8,128]{2,1,0:T(8,128)S(1)}, u32[]{:S(2)}, u32[]{:S(2)}) collective-permute-start(f32[8,8,128]{2,1,0:T(8,128)S(1)} %slice.25), channel_id=1, source_target_pairs={{0,8},{1,9},{2,10},{3,11},{4,12},{5,13},{6,14},{7,15},{8,0},{9,1},... | collective-permute-start | bytes 98312 | tf_op jit(solution)/shard_map/ppermute | solution.py:190
  51.8 4.1 %collective-permute-start.5 = (f32[4,8,128]{2,1,0:T(8,128)S(1)}, f32[4,8,128]{2,1,0:T(8,128)S(1)}, u32[]{:S(2)}, u32[]{:S(2)}) collective-permute-start(f32[4,8,128]{2,1,0:T(8,128)S(1)} %slice.33), channel_id=1, source_target_pairs={{0,4},{1,5},{2,6},{3,7},{4,0},{5,1},{6,2},{7,3},{8,12},{9,13},{10,... | collective-permute-start | bytes 49160 | tf_op jit(solution)/shard_map/ppermute | solution.py:190
  55.9 3.7 %collective-permute-start.6 = (f32[2,8,128]{2,1,0:T(8,128)S(1)}, f32[2,8,128]{2,1,0:T(8,128)S(1)}, u32[]{:S(2)}, u32[]{:S(2)}) collective-permute-start(f32[2,8,128]{2,1,0:T(8,128)S(1)} %slice.35), channel_id=1, source_target_pairs={{0,2},{1,3},{2,0},{3,1},{4,6},{5,7},{6,4},{7,5},{8,10},{9,11},{10,... | collective-permute-start | bytes 24584 | tf_op jit(solution)/shard_map/ppermute | solution.py:190
  59.6 1.2 %collective-permute-start.7 = (f32[1,8,128]{2,1,0:T(8,128)S(1)}, f32[1,8,128]{2,1,0:T(8,128)S(1)}, u32[]{:S(2)}, u32[]{:S(2)}) collective-permute-start(f32[1,8,128]{2,1,0:T(8,128)S(1)} %slice.37), channel_id=1, source_target_pairs={{0,1},{1,0},{2,3},{3,2},{4,5},{5,4},{6,7},{7,6},{8,9},{9,8},{10,11... | collective-permute-start | bytes 12296 | tf_op jit(solution)/shard_map/ppermute | solution.py:190

commit v2 on v1

v2 whole, which is shorter than its diff:
```python
import functools
import math

import jax
import jax.numpy as jnp
import numpy as np
from jax import lax
from jax.experimental import pallas as pl
from jax.experimental.pallas import tpu as pltpu
from jax.sharding import PartitionSpec as P

LANES = 128
WIDE = 256
ROWS = 16
DEPTH = 32
CELL_STEP = 256
SLOT_STEP = 512
KEEP_BYTES = 24 << 20


def fit(values, terms):
    nodes = 0.125 + 0.125 * np.cos(np.pi * (np.arange(64) + 0.5) / 64)
    series = np.polynomial.chebyshev.Chebyshev.fit(nodes, values(np.sqrt(nodes)), terms - 1, domain=[0.0, 0.25])
    all_of = series.convert(kind=np.polynomial.Polynomial).coef
    return [float(c / all_of[-1]) for c in all_of[:-1]], float(all_of[-1])


SINE, SINE_TOP = fit(lambda f: np.sin(0.5 * np.pi * f) / f, 3)
COSINE, COSINE_TOP = fit(lambda f: np.cos(0.5 * np.pi * f), 4)
HALF_COSINE = 2.0 * SINE_TOP * SINE_TOP
COS_UNIT = 2.0 ** round(math.log2(8.0 * (SINE_TOP * COSINE_TOP) ** 2))
HALF_SINE = math.sqrt(0.5 * COS_UNIT)
RATIO = 2.0 * SINE_TOP * COSINE_TOP / HALF_SINE
SIN_UNIT = 2.0 * HALF_SINE * HALF_COSINE


def series_of(u, top, coefficients):
    total = (u if top == 1.0 else top * u) + coefficients[-1]
    for c in coefficients[-2::-1]:
        total = total * u + c
    return total


def cos_sin(turns):
    f = turns - jnp.round(turns)
    u = f * f
    s = f * series_of(u, 1.0, SINE)
    c = series_of(u, RATIO, [RATIO * v for v in COSINE])
    half = s * c
    return 1.0 / COS_UNIT - half * half, half * (1.0 / HALF_COSINE - s * s)


def lookup_kernel(tri_ref, table_ref, out_ref):
    rows = table_ref.shape[0]
    width = tri_ref.shape[1]
    lane_iota = lax.broadcasted_iota(jnp.int32, (WIDE, width), 0)
    row_iota = lax.broadcasted_iota(jnp.int32, (rows, width), 0)
    table = table_ref[...]
    bytes_of = jnp.concatenate([table & 255, table - (table & 255)], axis=1)
    left = bytes_of.astype(jnp.float32).astype(jnp.bfloat16)
    for place in range(3):
        index = tri_ref[place : place + 1, :]
        pick = jnp.where(lane_iota == (index & (WIDE - 1)), 1.0, 0.0).astype(jnp.bfloat16)
        line = jnp.dot(left, jnp.concatenate([pick, pick], axis=0), preferred_element_type=jnp.float32)
        code = jnp.sum(jnp.where(row_iota == (index >> (WIDE.bit_length() - 1)), line, 0.0), axis=0, keepdims=True)
        third = jnp.floor(code * (1.0 / 1024.0))
        rest = code - 1024.0 * third
        second = jnp.floor(rest * (1.0 / 32.0))
        first = rest - 32.0 * second
        eight = jnp.concatenate([first + 1.0, second + 1.0, third + 1.0, jnp.zeros((5, width), jnp.float32)], axis=0)
        wide = jnp.concatenate([eight, eight, eight, jnp.zeros((LANES - 24, width), jnp.float32)], axis=0)
        out_ref[place * width : (place + 1) * width, :] = wide.T.astype(jnp.bfloat16)


def main_kernel(keep, norm, data_ref, slot_ref, cot_ref, corr_ref, grad_ref, x_ref, w_ref, sum_ref, cos_ref, sin_ref):
    blocks = data_ref.shape[0]
    slots = slot_ref.shape[0]
    width = cot_ref.shape[1]
    cells = blocks * LANES
    cell_steps = cells // CELL_STEP
    slot_steps = slots // SLOT_STEP
    per_step = CELL_STEP // LANES

    def prepare(j, carry):
        at = pl.ds(pl.multiple_of(j * LANES, LANES), LANES)
        place = data_ref[j, 0:8, :]
        place = place - jnp.round(place)
        high = place.astype(jnp.bfloat16).astype(jnp.float32)
        rest = place - high
        middle = rest.astype(jnp.bfloat16).astype(jnp.float32)
        low = rest - middle
        none = jnp.zeros_like(low)
        x_ref[:, at] = jnp.concatenate([high, middle, low, none], axis=0).astype(jnp.bfloat16)
        w_ref[:, at] = data_ref[j, 8:16, :].astype(jnp.bfloat16)
        return carry

    lax.fori_loop(0, blocks, prepare, 0)
    sum_ref[...] = jnp.zeros_like(sum_ref)

    def over_cells(left, right):
        return lax.dot_general(left, right, (((1,), (1,)), ((), ())), preferred_element_type=jnp.float32)

    def columns(step):
        return pl.ds(pl.multiple_of(step * CELL_STEP, CELL_STEP), CELL_STEP)

    def fill(step, slot_at, add):
        to = columns(slot_at)
        x = x_ref[:, columns(step)]
        weights = w_ref[:, columns(step)]

        def some(b, carry):
            here = pl.ds(pl.multiple_of(b * SLOT_STEP, SLOT_STEP), SLOT_STEP)
            turns = jnp.dot(slot_ref[here, 0:DEPTH], x, preferred_element_type=jnp.float32)
            c, s = cos_sin(turns)
            c, s = c.astype(jnp.bfloat16), s.astype(jnp.bfloat16)
            cos_ref[here, to] = c
            sin_ref[here, to] = s
            return carry

        lax.fori_loop(0, slot_steps, some, 0)
        if add and not keep:
            sum_ref[0:8, :] += over_cells(weights, cos_ref[:, to])
            sum_ref[8:16, :] += over_cells(weights, sin_ref[:, to])
        return to

    def forward(step, carry):
        fill(step, step if keep else 0, True)
        return carry

    lax.fori_loop(0, cell_steps, forward, 0)
    if keep:

        def total(b, carry):
            here = pl.ds(pl.multiple_of(b * SLOT_STEP, SLOT_STEP), SLOT_STEP)
            sum_ref[0:8, here] = over_cells(w_ref[...], cos_ref[here, :])
            sum_ref[8:16, here] = over_cells(w_ref[...], sin_ref[here, :])
            return carry

        lax.fori_loop(0, slot_steps, total, 0)
    real, imag = sum_ref[0:8, :] * (norm * COS_UNIT), sum_ref[8:16, :] * (norm * SIN_UNIT)
    ar, br, cr = (real[:, p * width : (p + 1) * width] for p in range(3))
    ai, bi, ci = (imag[:, p * width : (p + 1) * width] for p in range(3))
    cot = cot_ref[...]
    bcr, bci = br * cr - bi * ci, br * ci + bi * cr
    corr_ref[...] = ar * bcr - ai * bci
    acr, aci = ar * cr - ai * ci, ar * ci + ai * cr
    abr, abi = ar * br - ai * bi, ar * bi + ai * br
    scaled_real, scaled_imag = cot * (norm * COS_UNIT), cot * (-norm * SIN_UNIT)
    left_real = jnp.concatenate([scaled_real * t for t in (bcr, acr, abr)], axis=1).astype(jnp.bfloat16)
    left_imag = jnp.concatenate([scaled_imag * t for t in (bci, aci, abi)], axis=1).astype(jnp.bfloat16)

    def backward(step, carry):
        to = columns(step) if keep else fill(step, 0, False)
        out = jnp.dot(left_real, cos_ref[:, to], preferred_element_type=jnp.float32) + jnp.dot(
            left_imag, sin_ref[:, to], preferred_element_type=jnp.float32
        )
        for i in range(per_step):
            grad_ref[step * per_step + i] = out[:, i * LANES : (i + 1) * LANES]
        return carry

    lax.fori_loop(0, cell_steps, backward, 0)


def lookup(triplets, momenta):
    units = jnp.array([1, 32, 1024], jnp.int32)[:, None]
    codes = jnp.sum((momenta - 1) * units, axis=0)
    slots = 3 * triplets.shape[1]
    return pl.pallas_call(
        lookup_kernel, out_shape=jax.ShapeDtypeStruct((slots, LANES), jnp.bfloat16), name="lookup"
    )(triplets, codes.reshape(-1, WIDE))


def triplet_stage(data, slot_rows, cotangent):
    blocks = data.shape[0]
    slots = slot_rows.shape[0]
    cells = blocks * LANES
    keep = 4 * slots * cells <= KEEP_BYTES
    kept = cells if keep else CELL_STEP
    return pl.pallas_call(
        functools.partial(main_kernel, keep, 1.0 / math.sqrt(cells)),
        out_shape=(
            jax.ShapeDtypeStruct(cotangent.shape, jnp.float32),
            jax.ShapeDtypeStruct((blocks, 8, LANES), jnp.float32),
        ),
        scratch_shapes=[
            pltpu.VMEM((DEPTH, cells), jnp.bfloat16),
            pltpu.VMEM((8, cells), jnp.bfloat16),
            pltpu.VMEM((16, slots), jnp.float32),
            pltpu.VMEM((slots, kept), jnp.bfloat16),
            pltpu.VMEM((slots, kept), jnp.bfloat16),
        ],
        in_specs=[pl.BlockSpec(memory_space=pltpu.VMEM)] * 3,
        name="triplet_stage",
    )(data, slot_rows, cotangent)


def gather_cells(block, devices):
    return lax.all_to_all(jnp.broadcast_to(block[None], (devices,) + block.shape), "cell", 0, 0)


def reduce_cells(blocks):
    return lax.all_to_all(blocks, "cell", 0, 0).sum(0)


def on_device(momenta, positions, weights, triplets, cotangent):
    devices = lax.axis_size("cell")
    block = jnp.concatenate(
        [positions, jnp.zeros((5, positions.shape[1]), jnp.float32), weights.astype(jnp.float32)], axis=0
    )
    data = gather_cells(block, devices)
    slot_rows = lookup(triplets, momenta)
    correlation, partial = triplet_stage(data, slot_rows, cotangent)
    return correlation, reduce_cells(partial)


def solution(mesh):
    split = P(None, ("grp", "cell"))
    return jax.shard_map(
        on_device,
        mesh=mesh,
        in_specs=(P(), split, split, split, split),
        out_specs=(split, split),
        check_vma=False,
    )
```

time: 61.6 us -> 49.7 us (0.81)
  blocking collectives: 0 us -> 10.5 us
  waiting for transfers between devices: 12.8 us -> 2.46 us
  starting transfers between devices: 15 us -> 7.52 us
  Pallas kernels: 29.3 us -> 22 us
  other arithmetic: 1.45 us -> 3.43 us
    ppermute x8 -> x0, starting transfers between devices: 15 us -> none  [the longest x4 8.12 us: gather_cells(): held = jnp.concatenate([held, lax.ppermute(held, 'cell', pairs)], axis=0)]
    ppermute x8 -> x0, waiting for transfers between devices: 12.8 us -> none  [the longest x4 6.91 us: reduce_cells(): blocks = blocks[:stride] + lax.ppermute(blocks[stride:], 'cell', pairs)]
    all_to_all x0 -> x1, blocking collectives: none -> 10.5 us  [reduce_cells(): return lax.all_to_all(blocks, 'cell', 0, 0).sum(0)]
    all_to_all x0 -> x1, starting transfers between devices: none -> 7.52 us  [gather_cells(): lax.all_to_all(jnp.broadcast_to(block[None], (devices,) + block.shape), '...]
    pallas_call x1, Pallas kernels: 24.6 us -> 19.4 us  [triplet_stage(): pl.pallas_call(functools.partial(main_kernel, keep, 1.0 / math.sqrt(cells...]
    reduce_sum x0 -> x2, other arithmetic: none -> 2.67 us  [the longest x1 2.06 us: lookup(): codes = jnp.sum((momenta - 1) * units, axis=0)]
    all_to_all x0 -> x1, waiting for transfers between devices: none -> 2.46 us  [gather_cells(): lax.all_to_all(jnp.broadcast_to(block[None], (devices,) + block.shape), '...]
    pallas_call x1, Pallas kernels: 4.69 us -> 2.58 us  [lookup(): pl.pallas_call(lookup_kernel, out_shape=jax.ShapeDtypeStruct((slots, LANE...]
  transfers between devices with their start and end apart: 8 -> 1, of which waited for: 7 -> 1; matrix products, arithmetic and copies ran while one was open for 0% -> 6% of each run, Pallas kernels for 8% -> 5%
where the time goes in v2:
time: 49.7 us; the launch traced here: 49.3 us
  Pallas kernels  22 us (44%)
  blocking collectives  10.5 us (21%)
  starting transfers between devices  7.52 us (15%)
  other arithmetic  3.43 us (7%)
  local copies, waits for them, and re-layouts  2.78 us (6%)
  waiting for transfers between devices  2.46 us (5%)
  between operations  0.66 us (1%)
    pallas_call x1, Pallas kernels, triplet_stage(): pl.pallas_call(functools.partial(main_kernel, keep, 1.0 / math.sqrt(cells...  19.4 us
    all_to_all x1, blocking collectives, reduce_cells(): return lax.all_to_all(blocks, 'cell', 0, 0).sum(0)  10.5 us
    all_to_all x1, starting transfers between devices, gather_cells(): lax.all_to_all(jnp.broadcast_to(block[None], (devices,) + block.shape), '...  7.52 us
    pallas_call x1, Pallas kernels, lookup(): pl.pallas_call(lookup_kernel, out_shape=jax.ShapeDtypeStruct((slots, LANE...  2.58 us
    all_to_all x1, waiting for transfers between devices, gather_cells(): lax.all_to_all(jnp.broadcast_to(block[None], (devices,) + block.shape), '...  2.46 us
    reduce_sum x1, other arithmetic, lookup(): codes = jnp.sum((momenta - 1) * units, axis=0)  2.06 us
    unnamed x6, local copies, waits for them, and re-layouts  1.25 us
  transfers between devices with their start and end apart: 1, of which 1 were waited for; matrix products, arithmetic and copies ran while one was open for 6% of the time, Pallas kernels for 5%

profile of v2, /device:TPU:0, one launch (start us, length us, event | category | flops | bytes accessed | tf_op | source)
XLA Modules:
  0.0 49.3 jit_solution(15887864922157272236)
XLA Ops:
  0.6 0.7 %convert_element_type.3 = f32[8,128]{1,0:T(8,128)S(1)} convert(bf16[8,128]{1,0:T(8,128)(2,1)} %param.8) | non-fusion elementwise | flops 1024 | bytes 6144 | tf_op jit(solution)/shard_map/convert_element_type | solution.py:208
  1.3 0.0 copy-start.1
  1.3 0.1 pad.1.clone
  1.4 0.6 %copy-done.1 = f32[3,128]{1,0:T(4,128)S(1)} copy-done((f32[3,128]{1,0:T(4,128)S(1)}, f32[3,128]{1,0:T(4,128)}, u32[]{:S(2)}) %copy-start.1) | copy-done | bytes 1560
  2.0 0.1 pad_maximum_fusion
  2.1 0.7 %broadcast_in_dim.5 = f32[16,16,128]{2,1,0:T(8,128)} broadcast(f32[16,128]{1,0:T(8,128)S(1)} %pad_maximum_fusion), dimensions={1,2} | broadcast | bytes 139264 | tf_op jit(solution)/shard_map/broadcast_in_dim | solution.py:198
  2.7 0.0 copy-start.2
  2.7 7.5 %all-to-all-start = ((f32[16,16,128]{2,1,0:T(8,128)}), f32[16,16,128]{2,1,0:T(8,128)S(1)}, u32[]{:S(2)}, u32[]{:S(2)}) async-start(f32[16,16,128]{2,1,0:T(8,128)} %broadcast_in_dim.5), calls=%async_computation | async-start | bytes 262144 | tf_op jit(solution)/shard_map/all_to_all | solution.py:198
  10.3 0.0 copy-done.2
  10.3 2.1 %multiply_reduce_fusion = s32[65536]{0:T(1024)S(1)} fusion(s32[3,65536]{1,0:T(4,128)} %param.6, s32[3]{0:T(128)S(1)} %copy-done.2), kind=kLoop, calls=%fused_computation | loop fusion | flops 524288 | bytes 1048588 | tf_op jit(solution)/shard_map/reduce_sum | solution.py:166
  12.3 0.8 %reshape.9.table_ref = s32[256,256]{1,0:T(8,128)} reshape(s32[65536]{0:T(1024)S(1)} %multiply_reduce_fusion) | data formatting | bytes 524288 | tf_op jit(solution)/shard_map/reshape | solution.py:170
  13.1 2.6 %lookup.1.slot_ref = bf16[1536,128]{1,0:T(8,128)(2,1)} custom-call(s32[3,512]{1,0:T(4,128)} %tri_ref.1, s32[256,256]{1,0:T(8,128)} %reshape.9.table_ref), custom_call_target="tpu_custom_call" | custom-call | tf_op jit(solution)/shard_map/lookup/pallas_call | solution.py:168
  15.7 2.5 %all-to-all-done.data_ref = f32[16,16,128]{2,1,0:T(8,128)S(1)} async-done(((f32[16,16,128]{2,1,0:T(8,128)}), f32[16,16,128]{2,1,0:T(8,128)S(1)}, u32[]{:S(2)}, u32[]{:S(2)}) %all-to-all-start) | async-done | bytes 131104 | tf_op jit(solution)/shard_map/all_to_all | solution.py:198
  18.2 0.0 copy-start
  18.2 0.6 %copy-done = f32[16,16,128]{2,1,0:T(8,128)} copy-done((f32[16,16,128]{2,1,0:T(8,128)}, f32[16,16,128]{2,1,0:T(8,128)S(1)}, u32[]{:S(2)}) %copy-start) | copy-done | bytes 131096
  18.8 19.4 %triplet_stage.1 = (f32[8,512]{1,0:T(8,128)}, f32[16,8,128]{2,1,0:T(8,128)}) custom-call(f32[16,16,128]{2,1,0:T(8,128)} %copy-done, bf16[1536,128]{1,0:T(8,128)(2,1)} %lookup.1.slot_ref, f32[8,512]{1,0:T(8,128)} %cot_ref.1), custom_call_target="tpu_custom_call" | custom-call | tf_op jit(solution)/shard_map/triplet_stage/pallas_call | solution.py:179
  38.2 10.5 %all_to_all.10 = f32[16,8,128]{2,1,0:T(8,128)S(1)} all-to-all(f32[16,8,128]{2,1,0:T(8,128)} %get-tuple-element.5), channel_id=1, replica_groups=mesh['grp'=2,'cell'=16] {'cell'}, dimensions={0} | all-to-all | bytes 131072 | tf_op jit(solution)/shard_map/all_to_all | solution.py:202
  48.7 0.6 %reduce_sum.19 = f32[8,128]{1,0:T(8,128)} reduce(f32[16,8,128]{2,1,0:T(8,128)S(1)} %all_to_all.10, f32[]{:T(128)} %constant.4.clone.1), dimensions={0}, to_apply=%region_1.0 | reduce | flops 15360 | bytes 69636 | tf_op jit(solution)/shard_map/reduce_sum | solution.py:202
  (1 shorter events, 0.0 us)
Async XLA Ops:
  1.3 0.7 %copy-start.1 = (f32[3,128]{1,0:T(4,128)S(1)}, f32[3,128]{1,0:T(4,128)}, u32[]{:S(2)}) copy-start(f32[3,128]{1,0:T(4,128)} %param.7) | copy-start | bytes 4612
  2.7 7.5 %copy-start.2 = (s32[3]{0:T(128)S(1)}, s32[3]{0:T(128)}, u32[]{:S(2)}) copy-start(s32[3]{0:T(128)} %constant.10.clone) | copy-start | bytes 40
  2.7 15.4 %all-to-all-start = ((f32[16,16,128]{2,1,0:T(8,128)}), f32[16,16,128]{2,1,0:T(8,128)S(1)}, u32[]{:S(2)}, u32[]{:S(2)}) async-start(f32[16,16,128]{2,1,0:T(8,128)} %broadcast_in_dim.5), calls=%async_computation | async-start | bytes 262144 | tf_op jit(solution)/shard_map/all_to_all | solution.py:198
  18.2 0.6 %copy-start = (f32[16,16,128]{2,1,0:T(8,128)}, f32[16,16,128]{2,1,0:T(8,128)S(1)}, u32[]{:S(2)}) copy-start(f32[16,16,128]{2,1,0:T(8,128)S(1)} %all-to-all-done.data_ref) | copy-start | bytes 393220

commit v3 on v2

--- a/solution.py
+++ b/solution.py
@@ -13,8 +13,10 @@
 WIDE = 256
 ROWS = 16
 DEPTH = 32
-CELL_STEP = 256
-SLOT_STEP = 512
+CELL_STEP = 512
+SLOT_STEP = 1536
+SUM_STEP = 1536
+BACK_STEP = 2048
 KEEP_BYTES = 24 << 20
 
 
@@ -78,8 +80,9 @@
     width = cot_ref.shape[1]
     cells = blocks * LANES
     cell_steps = cells // CELL_STEP
-    slot_steps = slots // SLOT_STEP
-    per_step = CELL_STEP // LANES
+    slot_step = math.gcd(SLOT_STEP, slots)
+    sum_step = math.gcd(SUM_STEP, slots)
+    slot_steps = slots // slot_step
 
     def prepare(j, carry):
         at = pl.ds(pl.multiple_of(j * LANES, LANES), LANES)
@@ -109,7 +112,7 @@
         weights = w_ref[:, columns(step)]
 
         def some(b, carry):
-            here = pl.ds(pl.multiple_of(b * SLOT_STEP, SLOT_STEP), SLOT_STEP)
+            here = pl.ds(pl.multiple_of(b * slot_step, slot_step), slot_step)
             turns = jnp.dot(slot_ref[here, 0:DEPTH], x, preferred_element_type=jnp.float32)
             c, s = cos_sin(turns)
             c, s = c.astype(jnp.bfloat16), s.astype(jnp.bfloat16)
@@ -131,12 +134,12 @@
     if keep:
 
         def total(b, carry):
-            here = pl.ds(pl.multiple_of(b * SLOT_STEP, SLOT_STEP), SLOT_STEP)
+            here = pl.ds(pl.multiple_of(b * sum_step, sum_step), sum_step)
             sum_ref[0:8, here] = over_cells(w_ref[...], cos_ref[here, :])
             sum_ref[8:16, here] = over_cells(w_ref[...], sin_ref[here, :])
             return carry
 
-        lax.fori_loop(0, slot_steps, total, 0)
+        lax.fori_loop(0, slots // sum_step, total, 0)
     real, imag = sum_ref[0:8, :] * (norm * COS_UNIT), sum_ref[8:16, :] * (norm * SIN_UNIT)
     ar, br, cr = (real[:, p * width : (p + 1) * width] for p in range(3))
     ai, bi, ci = (imag[:, p * width : (p + 1) * width] for p in range(3))
@@ -149,8 +152,11 @@
     left_real = jnp.concatenate([scaled_real * t for t in (bcr, acr, abr)], axis=1).astype(jnp.bfloat16)
     left_imag = jnp.concatenate([scaled_imag * t for t in (bci, aci, abi)], axis=1).astype(jnp.bfloat16)
 
+    back_step = math.gcd(BACK_STEP, cells) if keep else CELL_STEP
+    per_step = back_step // LANES
+
     def backward(step, carry):
-        to = columns(step) if keep else fill(step, 0, False)
+        to = pl.ds(pl.multiple_of(step * back_step, back_step), back_step) if keep else fill(step, 0, False)
         out = jnp.dot(left_real, cos_ref[:, to], preferred_element_type=jnp.float32) + jnp.dot(
             left_imag, sin_ref[:, to], preferred_element_type=jnp.float32
         )
@@ -158,7 +164,7 @@
             grad_ref[step * per_step + i] = out[:, i * LANES : (i + 1) * LANES]
         return carry
 
-    lax.fori_loop(0, cell_steps, backward, 0)
+    lax.fori_loop(0, cells // back_step, backward, 0)
 
 
 def lookup(triplets, momenta):
@@ -194,20 +200,29 @@
     )(data, slot_rows, cotangent)
 
 
-def gather_cells(block, devices):
-    return lax.all_to_all(jnp.broadcast_to(block[None], (devices,) + block.shape), "cell", 0, 0)
-
-
 def reduce_cells(blocks):
     return lax.all_to_all(blocks, "cell", 0, 0).sum(0)
 
 
+def pack_kernel(place_ref, weight_ref, out_ref):
+    width = place_ref.shape[1]
+    block = jnp.concatenate(
+        [place_ref[...], jnp.zeros((5, width), jnp.float32), weight_ref[...].astype(jnp.float32)], axis=0
+    )
+    for i in range(out_ref.shape[0]):
+        out_ref[i] = block
+
+
+def pack(positions, weights, devices):
+    return pl.pallas_call(
+        pack_kernel, out_shape=jax.ShapeDtypeStruct((devices, ROWS, positions.shape[1]), jnp.float32), name="pack"
+    )(positions, weights)
+
+
 def on_device(momenta, positions, weights, triplets, cotangent):
     devices = lax.axis_size("cell")
-    block = jnp.concatenate(
-        [positions, jnp.zeros((5, positions.shape[1]), jnp.float32), weights.astype(jnp.float32)], axis=0
-    )
-    data = gather_cells(block, devices)
+    data = lax.all_to_all(pack(positions, weights, devices), "cell", 0, 0)
+    data = pltpu.with_memory_space_constraint(data, pltpu.VMEM)
     slot_rows = lookup(triplets, momenta)
     correlation, partial = triplet_stage(data, slot_rows, cotangent)
     return correlation, reduce_cells(partial)

time: 49.7 us -> 44.4 us (0.89)
  Pallas kernels: 22 us -> 19.5 us
  local copies, waits for them, and re-layouts: 2.78 us -> 0.78 us
  other arithmetic: 3.43 us -> 2.67 us
    pallas_call x1, Pallas kernels: 19.4 us -> 15.6 us  [triplet_stage(): pl.pallas_call(functools.partial(main_kernel, keep, 1.0 / math.sqrt(cells...]
    pallas_call x0 -> x1, Pallas kernels: none -> 1.34 us  [pack(): pl.pallas_call(pack_kernel, out_shape=jax.ShapeDtypeStruct((devices, ROWS...]
    unnamed x6 -> x2, local copies, waits for them, and re-layouts: 1.25 us -> 0.01 us
    convert_element_type x1 -> x0, other arithmetic: 0.68 us -> none  [on_device(): weights.astype(jnp.float32)]
    broadcast_in_dim x2 -> x0, local copies, waits for them, and re-layouts: 0.67 us -> none  [the longest x1 0.66 us: gather_cells(): jnp.broadcast_to(block[None], (devices,) + block.shape)]
  transfers between devices with their start and end apart: 1 -> 1, of which waited for: 1 -> 1; matrix products, arithmetic and copies ran while one was open for 6% -> 6% of each run, Pallas kernels for 5% -> 6%
where the time goes in v3:
time: 44.4 us; the launch traced here: 44 us
  Pallas kernels  19.5 us (44%)
  blocking collectives  10.4 us (23%)
  starting transfers between devices  7.52 us (17%)
  other arithmetic  2.67 us (6%)
  waiting for transfers between devices  2.47 us (6%)
  local copies, waits for them, and re-layouts  0.78 us (2%)
  between operations  0.65 us (1%)
    pallas_call x1, Pallas kernels, triplet_stage(): pl.pallas_call(functools.partial(main_kernel, keep, 1.0 / math.sqrt(cells...  15.6 us
    all_to_all x1, blocking collectives, reduce_cells(): return lax.all_to_all(blocks, 'cell', 0, 0).sum(0)  10.4 us
    all_to_all x1, starting transfers between devices, on_device(): data = lax.all_to_all(pack(positions, weights, devices), 'cell', 0, 0)  7.52 us
    pallas_call x1, Pallas kernels, lookup(): pl.pallas_call(lookup_kernel, out_shape=jax.ShapeDtypeStruct((slots, LANE...  2.58 us
    all_to_all x1, waiting for transfers between devices, on_device(): data = lax.all_to_all(pack(positions, weights, devices), 'cell', 0, 0)  2.47 us
    reduce_sum x1, other arithmetic, lookup(): codes = jnp.sum((momenta - 1) * units, axis=0)  2.06 us
    pallas_call x1, Pallas kernels, pack(): pl.pallas_call(pack_kernel, out_shape=jax.ShapeDtypeStruct((devices, ROWS...  1.34 us
  transfers between devices with their start and end apart: 1, of which 1 were waited for; matrix products, arithmetic and copies ran while one was open for 6% of the time, Pallas kernels for 6%

profile of v3, /device:TPU:0, one launch (start us, length us, event | category | flops | bytes accessed | tf_op | source)
XLA Modules:
  0.0 44.0 jit_solution(9593751399131341192)
XLA Ops:
  0.6 1.3 %pack.1 = f32[16,16,128]{2,1,0:T(8,128)} custom-call(f32[3,128]{1,0:T(4,128)} %place_ref.1, bf16[8,128]{1,0:T(8,128)(2,1)} %weight_ref.1), custom_call_target="tpu_custom_call" | custom-call | tf_op jit(solution)/shard_map/pack/pallas_call | solution.py:217
  2.0 0.0 copy-start
  2.0 7.5 %all-to-all-start = ((f32[16,16,128]{2,1,0:T(8,128)}), f32[16,16,128]{2,1,0:T(8,128)S(1)}, u32[]{:S(2)}, u32[]{:S(2)}) async-start(f32[16,16,128]{2,1,0:T(8,128)} %pack.1), calls=%async_computation | async-start | bytes 262144 | tf_op jit(solution)/shard_map/all_to_all | solution.py:224
  9.5 0.0 copy-done
  9.5 2.1 %multiply_reduce_fusion = s32[65536]{0:T(1024)S(1)} fusion(s32[3,65536]{1,0:T(4,128)} %param.6, s32[3]{0:T(128)S(1)} %copy-done), kind=kLoop, calls=%fused_computation | loop fusion | flops 524288 | bytes 1048588 | tf_op jit(solution)/shard_map/reduce_sum | solution.py:172
  11.6 0.8 %reshape.8.table_ref = s32[256,256]{1,0:T(8,128)} reshape(s32[65536]{0:T(1024)S(1)} %multiply_reduce_fusion) | data formatting | bytes 524288 | tf_op jit(solution)/shard_map/reshape | solution.py:176
  12.4 2.6 %lookup.1.slot_ref = bf16[1536,128]{1,0:T(8,128)(2,1)} custom-call(s32[3,512]{1,0:T(4,128)} %tri_ref.1, s32[256,256]{1,0:T(8,128)} %reshape.8.table_ref), custom_call_target="tpu_custom_call" | custom-call | tf_op jit(solution)/shard_map/lookup/pallas_call | solution.py:174
  14.9 2.5 %all-to-all-done.data_ref = f32[16,16,128]{2,1,0:T(8,128)S(1)} async-done(((f32[16,16,128]{2,1,0:T(8,128)}), f32[16,16,128]{2,1,0:T(8,128)S(1)}, u32[]{:S(2)}, u32[]{:S(2)}) %all-to-all-start) | async-done | bytes 131104 | tf_op jit(solution)/shard_map/all_to_all | solution.py:224
  17.4 15.6 %triplet_stage.1 = (f32[8,512]{1,0:T(8,128)}, f32[16,8,128]{2,1,0:T(8,128)}) custom-call(f32[16,16,128]{2,1,0:T(8,128)S(1)} %all-to-all-done.data_ref, bf16[1536,128]{1,0:T(8,128)(2,1)} %lookup.1.slot_ref, f32[8,512]{1,0:T(8,128)} %cot_ref.1), custom_call_target="tpu_custom_call" | custom-call | tf_op jit(solution)/shard_map/triplet_stage/pallas_call | solution.py:185
  33.0 10.4 %all_to_all.10 = f32[16,8,128]{2,1,0:T(8,128)S(1)} all-to-all(f32[16,8,128]{2,1,0:T(8,128)} %get-tuple-element.5), channel_id=1, replica_groups=mesh['grp'=2,'cell'=16] {'cell'}, dimensions={0} | all-to-all | bytes 131072 | tf_op jit(solution)/shard_map/all_to_all | solution.py:204
  43.4 0.6 %reduce_sum.19 = f32[8,128]{1,0:T(8,128)} reduce(f32[16,8,128]{2,1,0:T(8,128)S(1)} %all_to_all.10, f32[]{:T(128)} %constant.8.clone.1), dimensions={0}, to_apply=%region_1.0 | reduce | flops 15360 | bytes 69636 | tf_op jit(solution)/shard_map/reduce_sum | solution.py:204
Async XLA Ops:
  2.0 7.5 %copy-start = (s32[3]{0:T(128)S(1)}, s32[3]{0:T(128)}, u32[]{:S(2)}) copy-start(s32[3]{0:T(128)} %constant.9.clone) | copy-start | bytes 40
  2.0 15.4 %all-to-all-start = ((f32[16,16,128]{2,1,0:T(8,128)}), f32[16,16,128]{2,1,0:T(8,128)S(1)}, u32[]{:S(2)}, u32[]{:S(2)}) async-start(f32[16,16,128]{2,1,0:T(8,128)} %pack.1), calls=%async_computation | async-start | bytes 262144 | tf_op jit(solution)/shard_map/all_to_all | solution.py:224

commit v4 on v3

--- a/solution.py
+++ b/solution.py
@@ -11,11 +11,10 @@
 
 LANES = 128
 WIDE = 256
-ROWS = 16
-DEPTH = 32
-CELL_STEP = 512
+DEPTH = 16
+ROWS = 24
+CELL_STEP = 2048
 SLOT_STEP = 1536
-SUM_STEP = 1536
 BACK_STEP = 2048
 KEEP_BYTES = 24 << 20
 
@@ -69,8 +68,8 @@
         rest = code - 1024.0 * third
         second = jnp.floor(rest * (1.0 / 32.0))
         first = rest - 32.0 * second
-        eight = jnp.concatenate([first + 1.0, second + 1.0, third + 1.0, jnp.zeros((5, width), jnp.float32)], axis=0)
-        wide = jnp.concatenate([eight, eight, eight, jnp.zeros((LANES - 24, width), jnp.float32)], axis=0)
+        three = [first + 1.0, second + 1.0, third + 1.0]
+        wide = jnp.concatenate(three * 3 + [jnp.zeros((LANES - 9, width), jnp.float32)], axis=0)
         out_ref[place * width : (place + 1) * width, :] = wide.T.astype(jnp.bfloat16)
 
 
@@ -79,22 +78,15 @@
     slots = slot_ref.shape[0]
     width = cot_ref.shape[1]
     cells = blocks * LANES
-    cell_steps = cells // CELL_STEP
+    cell_step = math.gcd(CELL_STEP, cells)
+    cell_steps = cells // cell_step
     slot_step = math.gcd(SLOT_STEP, slots)
-    sum_step = math.gcd(SUM_STEP, slots)
     slot_steps = slots // slot_step
 
     def prepare(j, carry):
         at = pl.ds(pl.multiple_of(j * LANES, LANES), LANES)
-        place = data_ref[j, 0:8, :]
-        place = place - jnp.round(place)
-        high = place.astype(jnp.bfloat16).astype(jnp.float32)
-        rest = place - high
-        middle = rest.astype(jnp.bfloat16).astype(jnp.float32)
-        low = rest - middle
-        none = jnp.zeros_like(low)
-        x_ref[:, at] = jnp.concatenate([high, middle, low, none], axis=0).astype(jnp.bfloat16)
-        w_ref[:, at] = data_ref[j, 8:16, :].astype(jnp.bfloat16)
+        x_ref[:, at] = data_ref[j, 0:DEPTH, :]
+        w_ref[:, at] = data_ref[j, DEPTH:ROWS, :]
         return carry
 
     lax.fori_loop(0, blocks, prepare, 0)
@@ -104,7 +96,7 @@
         return lax.dot_general(left, right, (((1,), (1,)), ((), ())), preferred_element_type=jnp.float32)
 
     def columns(step):
-        return pl.ds(pl.multiple_of(step * CELL_STEP, CELL_STEP), CELL_STEP)
+        return pl.ds(pl.multiple_of(step * cell_step, cell_step), cell_step)
 
     def fill(step, slot_at, add):
         to = columns(slot_at)
@@ -118,12 +110,12 @@
             c, s = c.astype(jnp.bfloat16), s.astype(jnp.bfloat16)
             cos_ref[here, to] = c
             sin_ref[here, to] = s
+            if add:
+                sum_ref[0:8, here] += over_cells(weights, c)
+                sum_ref[8:16, here] += over_cells(weights, s)
             return carry
 
         lax.fori_loop(0, slot_steps, some, 0)
-        if add and not keep:
-            sum_ref[0:8, :] += over_cells(weights, cos_ref[:, to])
-            sum_ref[8:16, :] += over_cells(weights, sin_ref[:, to])
         return to
 
     def forward(step, carry):
@@ -131,15 +123,6 @@
         return carry
 
     lax.fori_loop(0, cell_steps, forward, 0)
-    if keep:
-
-        def total(b, carry):
-            here = pl.ds(pl.multiple_of(b * sum_step, sum_step), sum_step)
-            sum_ref[0:8, here] = over_cells(w_ref[...], cos_ref[here, :])
-            sum_ref[8:16, here] = over_cells(w_ref[...], sin_ref[here, :])
-            return carry
-
-        lax.fori_loop(0, slots // sum_step, total, 0)
     real, imag = sum_ref[0:8, :] * (norm * COS_UNIT), sum_ref[8:16, :] * (norm * SIN_UNIT)
     ar, br, cr = (real[:, p * width : (p + 1) * width] for p in range(3))
     ai, bi, ci = (imag[:, p * width : (p + 1) * width] for p in range(3))
@@ -152,7 +135,7 @@
     left_real = jnp.concatenate([scaled_real * t for t in (bcr, acr, abr)], axis=1).astype(jnp.bfloat16)
     left_imag = jnp.concatenate([scaled_imag * t for t in (bci, aci, abi)], axis=1).astype(jnp.bfloat16)
 
-    back_step = math.gcd(BACK_STEP, cells) if keep else CELL_STEP
+    back_step = math.gcd(BACK_STEP, cells) if keep else cell_step
     per_step = back_step // LANES
 
     def backward(step, carry):
@@ -181,7 +164,7 @@
     slots = slot_rows.shape[0]
     cells = blocks * LANES
     keep = 4 * slots * cells <= KEEP_BYTES
-    kept = cells if keep else CELL_STEP
+    kept = cells if keep else math.gcd(CELL_STEP, cells)
     return pl.pallas_call(
         functools.partial(main_kernel, keep, 1.0 / math.sqrt(cells)),
         out_shape=(
@@ -205,17 +188,21 @@
 
 
 def pack_kernel(place_ref, weight_ref, out_ref):
-    width = place_ref.shape[1]
-    block = jnp.concatenate(
-        [place_ref[...], jnp.zeros((5, width), jnp.float32), weight_ref[...].astype(jnp.float32)], axis=0
-    )
+    place = place_ref[...]
+    place = place - jnp.round(place)
+    high = place.astype(jnp.bfloat16).astype(jnp.float32)
+    rest = place - high
+    middle = rest.astype(jnp.bfloat16).astype(jnp.float32)
+    none = jnp.zeros((DEPTH - 9, place.shape[1]), jnp.float32)
+    rows = [high, middle, rest - middle, none, weight_ref[...].astype(jnp.float32)]
+    block = jnp.concatenate(rows, axis=0).astype(jnp.bfloat16)
     for i in range(out_ref.shape[0]):
         out_ref[i] = block
 
 
 def pack(positions, weights, devices):
     return pl.pallas_call(
-        pack_kernel, out_shape=jax.ShapeDtypeStruct((devices, ROWS, positions.shape[1]), jnp.float32), name="pack"
+        pack_kernel, out_shape=jax.ShapeDtypeStruct((devices, ROWS, positions.shape[1]), jnp.bfloat16), name="pack"
     )(positions, weights)
 
 

time: 44.4 us -> 41.3 us (0.930)
  Pallas kernels: 19.5 us -> 16.4 us
  blocking collectives: 10.4 us -> 11 us
  waiting for transfers between devices: 2.47 us -> 1.94 us
    pallas_call x1, Pallas kernels: 15.6 us -> 12.5 us  [triplet_stage(): pl.pallas_call(functools.partial(main_kernel, keep, 1.0 / math.sqrt(cells...]
    all_to_all x1, blocking collectives: 10.4 us -> 11 us  [reduce_cells(): return lax.all_to_all(blocks, 'cell', 0, 0).sum(0)]
    all_to_all x1, waiting for transfers between devices: 2.47 us -> 1.94 us  [on_device(): data = lax.all_to_all(pack(positions, weights, devices), 'cell', 0, 0)]
  transfers between devices with their start and end apart: 1 -> 1, of which waited for: 1 -> 1; matrix products, arithmetic and copies ran while one was open for 6% -> 7% of each run, Pallas kernels for 6% -> 6%
where the time goes in v4:
time: 41.3 us; the launch traced here: 40.9 us
  Pallas kernels  16.4 us (40%)
  blocking collectives  11 us (27%)
  starting transfers between devices  7.52 us (18%)
  other arithmetic  2.67 us (6%)
  waiting for transfers between devices  1.94 us (5%)
  local copies, waits for them, and re-layouts  0.78 us (2%)
  between operations  0.65 us (2%)
    pallas_call x1, Pallas kernels, triplet_stage(): pl.pallas_call(functools.partial(main_kernel, keep, 1.0 / math.sqrt(cells...  12.5 us
    all_to_all x1, blocking collectives, reduce_cells(): return lax.all_to_all(blocks, 'cell', 0, 0).sum(0)  11 us
    all_to_all x1, starting transfers between devices, on_device(): data = lax.all_to_all(pack(positions, weights, devices), 'cell', 0, 0)  7.52 us
    pallas_call x1, Pallas kernels, lookup(): pl.pallas_call(lookup_kernel, out_shape=jax.ShapeDtypeStruct((slots, LANE...  2.58 us
    reduce_sum x1, other arithmetic, lookup(): codes = jnp.sum((momenta - 1) * units, axis=0)  2.06 us
    all_to_all x1, waiting for transfers between devices, on_device(): data = lax.all_to_all(pack(positions, weights, devices), 'cell', 0, 0)  1.94 us
    pallas_call x1, Pallas kernels, pack(): pl.pallas_call(pack_kernel, out_shape=jax.ShapeDtypeStruct((devices, ROWS...  1.35 us
  transfers between devices with their start and end apart: 1, of which 1 were waited for; matrix products, arithmetic and copies ran while one was open for 7% of the time, Pallas kernels for 6%

profile of v4, /device:TPU:0, one launch (start us, length us, event | category | flops | bytes accessed | tf_op | source)
XLA Modules:
  0.0 40.9 jit_solution(545148385254574852)
XLA Ops:
  0.6 1.4 %pack.1 = bf16[16,24,128]{2,1,0:T(8,128)(2,1)} custom-call(f32[3,128]{1,0:T(4,128)} %place_ref.1, bf16[8,128]{1,0:T(8,128)(2,1)} %weight_ref.1), custom_call_target="tpu_custom_call" | custom-call | tf_op jit(solution)/shard_map/pack/pallas_call | solution.py:204
  2.0 0.0 copy-start
  2.0 7.5 %all-to-all-start = ((bf16[16,24,128]{2,1,0:T(8,128)(2,1)}), bf16[16,24,128]{2,1,0:T(8,128)(2,1)S(1)}, u32[]{:S(2)}, u32[]{:S(2)}) async-start(bf16[16,24,128]{2,1,0:T(8,128)(2,1)} %pack.1), calls=%async_computation | async-start | bytes 196608 | tf_op jit(solution)/shard_map/all_to_all | solution.py:211
  9.5 0.0 copy-done
  9.5 2.1 %multiply_reduce_fusion = s32[65536]{0:T(1024)S(1)} fusion(s32[3,65536]{1,0:T(4,128)} %param.6, s32[3]{0:T(128)S(1)} %copy-done), kind=kLoop, calls=%fused_computation | loop fusion | flops 524288 | bytes 1048588 | tf_op jit(solution)/shard_map/reduce_sum | solution.py:155
  11.6 0.8 %reshape.8.table_ref = s32[256,256]{1,0:T(8,128)} reshape(s32[65536]{0:T(1024)S(1)} %multiply_reduce_fusion) | data formatting | bytes 524288 | tf_op jit(solution)/shard_map/reshape | solution.py:159
  12.4 2.6 %lookup.1.slot_ref = bf16[1536,128]{1,0:T(8,128)(2,1)} custom-call(s32[3,512]{1,0:T(4,128)} %tri_ref.1, s32[256,256]{1,0:T(8,128)} %reshape.8.table_ref), custom_call_target="tpu_custom_call" | custom-call | tf_op jit(solution)/shard_map/lookup/pallas_call | solution.py:157
  14.9 1.9 %all-to-all-done.data_ref = bf16[16,24,128]{2,1,0:T(8,128)(2,1)S(1)} async-done(((bf16[16,24,128]{2,1,0:T(8,128)(2,1)}), bf16[16,24,128]{2,1,0:T(8,128)(2,1)S(1)}, u32[]{:S(2)}, u32[]{:S(2)}) %all-to-all-start) | async-done | bytes 98336 | tf_op jit(solution)/shard_map/all_to_all | solution.py:211
  16.9 12.5 %triplet_stage.1 = (f32[8,512]{1,0:T(8,128)}, f32[16,8,128]{2,1,0:T(8,128)}) custom-call(bf16[16,24,128]{2,1,0:T(8,128)(2,1)S(1)} %all-to-all-done.data_ref, bf16[1536,128]{1,0:T(8,128)(2,1)} %lookup.1.slot_ref, f32[8,512]{1,0:T(8,128)} %cot_ref.1), custom_call_target="tpu_custom_call" | custom-call | tf_op jit(solution)/shard_map/triplet_stage/pallas_call | solution.py:168
  29.4 11.0 %all_to_all.10 = f32[16,8,128]{2,1,0:T(8,128)S(1)} all-to-all(f32[16,8,128]{2,1,0:T(8,128)} %get-tuple-element.5), channel_id=1, replica_groups=mesh['grp'=2,'cell'=16] {'cell'}, dimensions={0} | all-to-all | bytes 131072 | tf_op jit(solution)/shard_map/all_to_all | solution.py:187
  40.3 0.6 %reduce_sum.19 = f32[8,128]{1,0:T(8,128)} reduce(f32[16,8,128]{2,1,0:T(8,128)S(1)} %all_to_all.10, f32[]{:T(128)} %constant.8.clone.1), dimensions={0}, to_apply=%region_1.0 | reduce | flops 15360 | bytes 69636 | tf_op jit(solution)/shard_map/reduce_sum | solution.py:187
Async XLA Ops:
  2.0 7.5 %copy-start = (s32[3]{0:T(128)S(1)}, s32[3]{0:T(128)}, u32[]{:S(2)}) copy-start(s32[3]{0:T(128)} %constant.9.clone) | copy-start | bytes 40
  2.0 14.9 %all-to-all-start = ((bf16[16,24,128]{2,1,0:T(8,128)(2,1)}), bf16[16,24,128]{2,1,0:T(8,128)(2,1)S(1)}, u32[]{:S(2)}, u32[]{:S(2)}) async-start(bf16[16,24,128]{2,1,0:T(8,128)(2,1)} %pack.1), calls=%async_computation | async-start | bytes 196608 | tf_op jit(solution)/shard_map/all_to_all | solution.py:211

commit v5 on v4

--- a/solution.py
+++ b/solution.py
@@ -169,7 +169,7 @@
         functools.partial(main_kernel, keep, 1.0 / math.sqrt(cells)),
         out_shape=(
             jax.ShapeDtypeStruct(cotangent.shape, jnp.float32),
-            jax.ShapeDtypeStruct((blocks, 8, LANES), jnp.float32),
+            pltpu.VMEM((blocks, 8, LANES), jnp.float32),
         ),
         scratch_shapes=[
             pltpu.VMEM((DEPTH, cells), jnp.bfloat16),

time: 41.3 us -> 41 us (level)
  no operation moved by 1% of the time
where the time goes in v5:
time: 41 us; the launch traced here: 40.6 us
  Pallas kernels  16.3 us (40%)
  blocking collectives  10.8 us (26%)
  starting transfers between devices  7.52 us (18%)
  other arithmetic  2.67 us (7%)
  waiting for transfers between devices  1.94 us (5%)
  local copies, waits for them, and re-layouts  0.78 us (2%)
  between operations  0.65 us (2%)
    pallas_call x1, Pallas kernels, triplet_stage(): pl.pallas_call(functools.partial(main_kernel, keep, 1.0 / math.sqrt(cells...  12.4 us
    all_to_all x1, blocking collectives, reduce_cells(): return lax.all_to_all(blocks, 'cell', 0, 0).sum(0)  10.8 us
    all_to_all x1, starting transfers between devices, on_device(): data = lax.all_to_all(pack(positions, weights, devices), 'cell', 0, 0)  7.52 us
    pallas_call x1, Pallas kernels, lookup(): pl.pallas_call(lookup_kernel, out_shape=jax.ShapeDtypeStruct((slots, LANE...  2.58 us
    reduce_sum x1, other arithmetic, lookup(): codes = jnp.sum((momenta - 1) * units, axis=0)  2.06 us
    all_to_all x1, waiting for transfers between devices, on_device(): data = lax.all_to_all(pack(positions, weights, devices), 'cell', 0, 0)  1.94 us
    pallas_call x1, Pallas kernels, pack(): pl.pallas_call(pack_kernel, out_shape=jax.ShapeDtypeStruct((devices, ROWS...  1.35 us
  transfers between devices with their start and end apart: 1, of which 1 were waited for; matrix products, arithmetic and copies ran while one was open for 7% of the time, Pallas kernels for 6%

profile of v5, /device:TPU:0, one launch (start us, length us, event | category | flops | bytes accessed | tf_op | source)
XLA Modules:
  0.0 40.6 jit_solution(16912171654925908181)
XLA Ops:
  0.6 1.4 %pack.1 = bf16[16,24,128]{2,1,0:T(8,128)(2,1)} custom-call(f32[3,128]{1,0:T(4,128)} %place_ref.1, bf16[8,128]{1,0:T(8,128)(2,1)} %weight_ref.1), custom_call_target="tpu_custom_call" | custom-call | tf_op jit(solution)/shard_map/pack/pallas_call | solution.py:204
  2.0 0.0 copy-start
  2.0 7.5 %all-to-all-start = ((bf16[16,24,128]{2,1,0:T(8,128)(2,1)}), bf16[16,24,128]{2,1,0:T(8,128)(2,1)S(1)}, u32[]{:S(2)}, u32[]{:S(2)}) async-start(bf16[16,24,128]{2,1,0:T(8,128)(2,1)} %pack.1), calls=%async_computation | async-start | bytes 196608 | tf_op jit(solution)/shard_map/all_to_all | solution.py:211
  9.5 0.0 copy-done
  9.5 2.1 %multiply_reduce_fusion = s32[65536]{0:T(1024)S(1)} fusion(s32[3,65536]{1,0:T(4,128)} %param.6, s32[3]{0:T(128)S(1)} %copy-done), kind=kLoop, calls=%fused_computation | loop fusion | flops 524288 | bytes 1048588 | tf_op jit(solution)/shard_map/reduce_sum | solution.py:155
  11.6 0.8 %reshape.8.table_ref = s32[256,256]{1,0:T(8,128)} reshape(s32[65536]{0:T(1024)S(1)} %multiply_reduce_fusion) | data formatting | bytes 524288 | tf_op jit(solution)/shard_map/reshape | solution.py:159
  12.4 2.6 %lookup.1.slot_ref = bf16[1536,128]{1,0:T(8,128)(2,1)} custom-call(s32[3,512]{1,0:T(4,128)} %tri_ref.1, s32[256,256]{1,0:T(8,128)} %reshape.8.table_ref), custom_call_target="tpu_custom_call" | custom-call | tf_op jit(solution)/shard_map/lookup/pallas_call | solution.py:157
  14.9 1.9 %all-to-all-done.data_ref = bf16[16,24,128]{2,1,0:T(8,128)(2,1)S(1)} async-done(((bf16[16,24,128]{2,1,0:T(8,128)(2,1)}), bf16[16,24,128]{2,1,0:T(8,128)(2,1)S(1)}, u32[]{:S(2)}, u32[]{:S(2)}) %all-to-all-start) | async-done | bytes 98336 | tf_op jit(solution)/shard_map/all_to_all | solution.py:211
  16.9 12.4 %triplet_stage.1 = (f32[8,512]{1,0:T(8,128)}, f32[16,8,128]{2,1,0:T(8,128)S(1)}) custom-call(bf16[16,24,128]{2,1,0:T(8,128)(2,1)S(1)} %all-to-all-done.data_ref, bf16[1536,128]{1,0:T(8,128)(2,1)} %lookup.1.slot_ref, f32[8,512]{1,0:T(8,128)} %cot_ref.1), custom_call_target="tpu_custom_call" | custom-call | tf_op jit(solution)/shard_map/triplet_stage/pallas_call | solution.py:168
  29.2 10.8 %all_to_all.10 = f32[16,8,128]{2,1,0:T(8,128)S(1)} all-to-all(f32[16,8,128]{2,1,0:T(8,128)S(1)} %get-tuple-element.5), channel_id=1, replica_groups=mesh['grp'=2,'cell'=16] {'cell'}, dimensions={0} | all-to-all | bytes 131072 | tf_op jit(solution)/shard_map/all_to_all | solution.py:187
  40.0 0.6 %reduce_sum.19 = f32[8,128]{1,0:T(8,128)} reduce(f32[16,8,128]{2,1,0:T(8,128)S(1)} %all_to_all.10, f32[]{:T(128)} %constant.8.clone.1), dimensions={0}, to_apply=%region_1.0 | reduce | flops 15360 | bytes 69636 | tf_op jit(solution)/shard_map/reduce_sum | solution.py:187
Async XLA Ops:
  2.0 7.5 %copy-start = (s32[3]{0:T(128)S(1)}, s32[3]{0:T(128)}, u32[]{:S(2)}) copy-start(s32[3]{0:T(128)} %constant.9.clone) | copy-start | bytes 40
  2.0 14.9 %all-to-all-start = ((bf16[16,24,128]{2,1,0:T(8,128)(2,1)}), bf16[16,24,128]{2,1,0:T(8,128)(2,1)S(1)}, u32[]{:S(2)}, u32[]{:S(2)}) async-start(bf16[16,24,128]{2,1,0:T(8,128)(2,1)} %pack.1), calls=%async_computation | async-start | bytes 196608 | tf_op jit(solution)/shard_map/all_to_all | solution.py:211

commit v6 on v5

--- a/solution.py
+++ b/solution.py
@@ -155,7 +155,7 @@
     codes = jnp.sum((momenta - 1) * units, axis=0)
     slots = 3 * triplets.shape[1]
     return pl.pallas_call(
-        lookup_kernel, out_shape=jax.ShapeDtypeStruct((slots, LANES), jnp.bfloat16), name="lookup"
+        lookup_kernel, out_shape=pltpu.VMEM((slots, LANES), jnp.bfloat16), name="lookup"
     )(triplets, codes.reshape(-1, WIDE))
 
 
@@ -210,7 +210,7 @@
     devices = lax.axis_size("cell")
     data = lax.all_to_all(pack(positions, weights, devices), "cell", 0, 0)
     data = pltpu.with_memory_space_constraint(data, pltpu.VMEM)
-    slot_rows = lookup(triplets, momenta)
+    slot_rows = pltpu.with_memory_space_constraint(lookup(triplets, momenta), pltpu.VMEM)
     correlation, partial = triplet_stage(data, slot_rows, cotangent)
     return correlation, reduce_cells(partial)
 

time: 41 us -> 40 us (0.976)
  Pallas kernels: 16.3 us -> 15.3 us
  blocking collectives: 10.8 us -> 10 us
  waiting for transfers between devices: 1.94 us -> 2.69 us
    pallas_call x1, Pallas kernels: 2.58 us -> 1.84 us  [lookup(): pl.pallas_call(lookup_kernel, out_shape=pltpu.VMEM((slots, LANES), jnp.bf...]
    all_to_all x1, waiting for transfers between devices: 1.94 us -> 2.69 us  [on_device(): data = lax.all_to_all(pack(positions, weights, devices), 'cell', 0, 0)]
    all_to_all x1, blocking collectives: 10.8 us -> 10 us  [reduce_cells(): return lax.all_to_all(blocks, 'cell', 0, 0).sum(0)]
  transfers between devices with their start and end apart: 1 -> 1, of which waited for: 1 -> 1; matrix products, arithmetic and copies ran while one was open for 7% -> 7% of each run, Pallas kernels for 6% -> 5%
where the time goes in v6:
time: 40 us; the launch traced here: 39.6 us
  Pallas kernels  15.3 us (38%)
  blocking collectives  10 us (25%)
  starting transfers between devices  7.52 us (19%)
  waiting for transfers between devices  2.69 us (7%)
  other arithmetic  2.67 us (7%)
  local copies, waits for them, and re-layouts  0.77 us (2%)
  between operations  0.66 us (2%)
    pallas_call x1, Pallas kernels, triplet_stage(): pl.pallas_call(functools.partial(main_kernel, keep, 1.0 / math.sqrt(cells...  12.1 us
    all_to_all x1, blocking collectives, reduce_cells(): return lax.all_to_all(blocks, 'cell', 0, 0).sum(0)  10 us
    all_to_all x1, starting transfers between devices, on_device(): data = lax.all_to_all(pack(positions, weights, devices), 'cell', 0, 0)  7.52 us
    all_to_all x1, waiting for transfers between devices, on_device(): data = lax.all_to_all(pack(positions, weights, devices), 'cell', 0, 0)  2.69 us
    reduce_sum x1, other arithmetic, lookup(): codes = jnp.sum((momenta - 1) * units, axis=0)  2.06 us
    pallas_call x1, Pallas kernels, lookup(): pl.pallas_call(lookup_kernel, out_shape=pltpu.VMEM((slots, LANES), jnp.bf...  1.84 us
    pallas_call x1, Pallas kernels, pack(): pl.pallas_call(pack_kernel, out_shape=jax.ShapeDtypeStruct((devices, ROWS...  1.36 us
  transfers between devices with their start and end apart: 1, of which 1 were waited for; matrix products, arithmetic and copies ran while one was open for 7% of the time, Pallas kernels for 5%

profile of v6, /device:TPU:0, one launch (start us, length us, event | category | flops | bytes accessed | tf_op | source)
XLA Modules:
  0.0 39.6 jit_solution(11218920153072319215)
XLA Ops:
  0.6 1.4 %pack.1 = bf16[16,24,128]{2,1,0:T(8,128)(2,1)} custom-call(f32[3,128]{1,0:T(4,128)} %place_ref.1, bf16[8,128]{1,0:T(8,128)(2,1)} %weight_ref.1), custom_call_target="tpu_custom_call" | custom-call | tf_op jit(solution)/shard_map/pack/pallas_call | solution.py:204
  2.0 0.0 copy-start
  2.0 7.5 %all-to-all-start = ((bf16[16,24,128]{2,1,0:T(8,128)(2,1)}), bf16[16,24,128]{2,1,0:T(8,128)(2,1)S(1)}, u32[]{:S(2)}, u32[]{:S(2)}) async-start(bf16[16,24,128]{2,1,0:T(8,128)(2,1)} %pack.1), calls=%async_computation | async-start | bytes 196608 | tf_op jit(solution)/shard_map/all_to_all | solution.py:211
  9.5 0.0 copy-done
  9.5 2.1 %multiply_reduce_fusion = s32[65536]{0:T(1024)S(1)} fusion(s32[3,65536]{1,0:T(4,128)} %param.6, s32[3]{0:T(128)S(1)} %copy-done), kind=kLoop, calls=%fused_computation | loop fusion | flops 524288 | bytes 1048588 | tf_op jit(solution)/shard_map/reduce_sum | solution.py:155
  11.6 0.8 %reshape.8.table_ref = s32[256,256]{1,0:T(8,128)} reshape(s32[65536]{0:T(1024)S(1)} %multiply_reduce_fusion) | data formatting | bytes 524288 | tf_op jit(solution)/shard_map/reshape | solution.py:159
  12.4 1.8 %lookup.1.slot_ref = bf16[1536,128]{1,0:T(8,128)(2,1)S(1)} custom-call(s32[3,512]{1,0:T(4,128)} %tri_ref.1, s32[256,256]{1,0:T(8,128)} %reshape.8.table_ref), custom_call_target="tpu_custom_call" | custom-call | tf_op jit(solution)/shard_map/lookup/pallas_call | solution.py:157
  14.2 2.7 %all-to-all-done.data_ref = bf16[16,24,128]{2,1,0:T(8,128)(2,1)S(1)} async-done(((bf16[16,24,128]{2,1,0:T(8,128)(2,1)}), bf16[16,24,128]{2,1,0:T(8,128)(2,1)S(1)}, u32[]{:S(2)}, u32[]{:S(2)}) %all-to-all-start) | async-done | bytes 98336 | tf_op jit(solution)/shard_map/all_to_all | solution.py:211
  16.9 12.1 %triplet_stage.1 = (f32[8,512]{1,0:T(8,128)}, f32[16,8,128]{2,1,0:T(8,128)S(1)}) custom-call(bf16[16,24,128]{2,1,0:T(8,128)(2,1)S(1)} %all-to-all-done.data_ref, bf16[1536,128]{1,0:T(8,128)(2,1)S(1)} %lookup.1.slot_ref, f32[8,512]{1,0:T(8,128)} %cot_ref.1), custom_call_target="tpu_custom_call" | custom-call | tf_op jit(solution)/shard_map/triplet_stage/pallas_call | solution.py:168
  29.0 10.0 %all_to_all.10 = f32[16,8,128]{2,1,0:T(8,128)S(1)} all-to-all(f32[16,8,128]{2,1,0:T(8,128)S(1)} %get-tuple-element.5), channel_id=1, replica_groups=mesh['grp'=2,'cell'=16] {'cell'}, dimensions={0} | all-to-all | bytes 131072 | tf_op jit(solution)/shard_map/all_to_all | solution.py:187
  39.0 0.6 %reduce_sum.19 = f32[8,128]{1,0:T(8,128)} reduce(f32[16,8,128]{2,1,0:T(8,128)S(1)} %all_to_all.10, f32[]{:T(128)} %constant.8.clone.1), dimensions={0}, to_apply=%region_1.0 | reduce | flops 15360 | bytes 69636 | tf_op jit(solution)/shard_map/reduce_sum | solution.py:187
Async XLA Ops:
  2.0 7.5 %copy-start = (s32[3]{0:T(128)S(1)}, s32[3]{0:T(128)}, u32[]{:S(2)}) copy-start(s32[3]{0:T(128)} %constant.9.clone) | copy-start | bytes 40
  2.0 14.9 %all-to-all-start = ((bf16[16,24,128]{2,1,0:T(8,128)(2,1)}), bf16[16,24,128]{2,1,0:T(8,128)(2,1)S(1)}, u32[]{:S(2)}, u32[]{:S(2)}) async-start(bf16[16,24,128]{2,1,0:T(8,128)(2,1)} %pack.1), calls=%async_computation | async-start | bytes 196608 | tf_op jit(solution)/shard_map/all_to_all | solution.py:211
